TPU v7x, 256 devices: a whole 4x4x8 slice. The times are simulated.
256 devices in a mesh: leaf: 64 (over z, x, core), level: 4 (over y).
Axes of the slice: x: 4, y: 4, z: 8, core: 2. Of those that a mesh axis runs over, the one named last changes fastest.
Arguments:
- charges: bfloat16 [3072, 128, 256], P(('leaf', 'level')), may hold values from -6 to 6
- near_mat: bfloat16 [3072, 16, 128, 128], P(('leaf', 'level')), may hold values from -0.1875 to 0.1875
- near_source: int32 [3072, 16], P(('leaf', 'level')), may hold values from 0 to 143
- near_count: int32 [3072], P(('leaf', 'level')), may hold values from 1 to 16, as said below
- moment_map: bfloat16 [3072, 256, 128], P(('leaf', 'level')), may hold values from -0.078125 to 0.078125
- local_eval: bfloat16 [3072, 128, 256], P(('leaf', 'level')), may hold values from -0.375 to 0.375
- upward_child_translation: bfloat16 [8, 256, 256], replicated, may hold values from -0.125 to 0.125
- shift_down: bfloat16 [8, 256, 256], replicated, may hold values from -0.375 to 0.375
- transfer_ops: bfloat16 [8, 256, 256], replicated, may hold values from -0.0625 to 0.0625
- subtree_interaction_list: int32 [64, 32], P('leaf'), may hold values from 0 to 63
- subtree_interaction_operators: int32 [64, 32], P('leaf'), may hold values from 0 to 7
- parent_list: int32 [64, 8], P('leaf'), may hold values from 0 to 7
- parent_ops: int32 [64, 8], P('leaf'), may hold values from 0 to 7
Outputs:
- potential: float32 [3072, 128, 256], P(('leaf', 'level'))
Inputs may be any that keep to these rules, and one draw needn't show every extreme that they name: `near_count`: some block uses all 16 slots and some block only one.
All inputs are finite; a program needn't handle non-finite values.
Results may differ from a plain program's by a relative error of at most 0.012.
Values may be sent and summed in bfloat16 or wider, within the bound.
No kernel may reach another device: no remote copies, remote signals or barrier semaphores. Data moves between devices by JAX's collectives and lax.ppermute only.
A program may use at most 128 MiB of HBM per device.

v0:
```python
import jax
import jax.numpy as jnp
from jax import lax
from jax.sharding import PartitionSpec as P


def extended_2(cells, sides, width):
    for axis, dim in sides:
        count = lax.axis_size(axis)
        ends = count - 1
        head = lax.slice_in_dim(cells, 0, width, axis=dim)
        tail = lax.slice_in_dim(cells, cells.shape[dim] - width, cells.shape[dim], axis=dim)
        cells = jnp.concatenate(
            [
                lax.ppermute(tail, axis, [(i, (i + 1) % count) for i in range(ends)]),
                cells,
                lax.ppermute(head, axis, [((i + 1) % count, i) for i in range(ends)]),
            ],
            axis=dim,
        )
    return cells


def top_tree(
    every,
    upward_child_translation,
    shift_down,
    transfer_ops,
    subtree_interaction_list,
    subtree_interaction_operators,
    parent_list,
    parent_ops,
    leaf_index,
):
    leaves, coeffs, columns = every.shape
    grouped_terms = every.reshape(leaves // 8, 8, coeffs, columns)
    upper_levels = jnp.einsum(
        "get,kgtv->kev", upward_child_translation, grouped_terms, preferred_element_type=jnp.float32
    ).astype(jnp.bfloat16)
    coarse = jnp.einsum(
        "kcd,kdr->cr",
        transfer_ops[parent_ops[0]],
        upper_levels[parent_list[0]],
        preferred_element_type=jnp.float32,
    ).astype(jnp.bfloat16)
    far_leaf = jnp.einsum(
        "kcd,kdr->cr",
        transfer_ops[subtree_interaction_operators[0]],
        every[subtree_interaction_list[0]],
        preferred_element_type=jnp.float32,
    )
    downward = jnp.dot(shift_down[leaf_index % 8], coarse, preferred_element_type=jnp.float32)
    return (far_leaf + downward).astype(jnp.bfloat16)


def on_device(
    charges,
    near_mat,
    near_source,
    near_count,
    moment_map,
    local_eval,
    upward_child_translation,
    shift_down,
    transfer_ops,
    subtree_interaction_list,
    subtree_interaction_operators,
    parent_list,
    parent_ops,
):
    slots = near_mat.shape[1]
    subtree = lax.all_gather(charges, "level", axis=0, tiled=True)
    extended = extended_2(subtree, (("leaf", 0),), subtree.shape[0])
    picked = extended[near_source]
    active = (jnp.arange(slots, dtype=jnp.int32)[None, :] < near_count[:, None]).astype(
        jnp.bfloat16
    )
    picked = picked * active[:, :, None, None]
    near_part = jnp.einsum("bkpq,bkqr->bpr", near_mat, picked, preferred_element_type=jnp.float32)
    partial_moment = jnp.einsum(
        "bcp,bpr->cr", moment_map, charges, preferred_element_type=jnp.float32
    )
    leaf_index = lax.axis_index("leaf")
    moment = lax.psum(partial_moment.astype(jnp.bfloat16), "level")
    every = lax.all_gather(moment[None], "leaf", axis=0, tiled=True)
    local_part = top_tree(
        every,
        upward_child_translation,
        shift_down,
        transfer_ops,
        subtree_interaction_list,
        subtree_interaction_operators,
        parent_list,
        parent_ops,
        leaf_index,
    )
    far_part = jnp.einsum("bpc,cr->bpr", local_eval, local_part, preferred_element_type=jnp.float32)
    return near_part + far_part


def solution(mesh):
    placed = (
        P(("leaf", "level"), None, None),
        P(("leaf", "level"), None, None, None),
        P(("leaf", "level"), None),
        P(("leaf", "level")),
        P(("leaf", "level"), None, None),
        P(("leaf", "level"), None, None),
        P(),
        P(),
        P(),
        P("leaf", None),
        P("leaf", None),
        P("leaf", None),
        P("leaf", None),
    )
    return jax.shard_map(
        on_device,
        mesh=mesh,
        in_specs=placed,
        out_specs=P(("leaf", "level"), None, None),
        check_vma=False,
    )
```

profile of v0, /device:TPU:103, one launch (start us, length us, event | category | flops | bytes accessed | tf_op | source)
XLA Modules:
  0.0 231.8 jit_solution(3247410838116859868)
XLA Ops:
  6.5 2.5 %fusion.10 = bf16[1,256,256]{2,1,0:T(8,128)(2,1)} fusion(bf16[12,256,128]{2,1,0:T(8,128)(2,1)} %param.17, bf16[12,128,256]{2,1,0:T(8,128)(2,1)} %param.13), kind=kOutput, calls=%fused_computation.20 | convolution fusion | flops 201392128 | bytes 1703936 | tf_op jit(solution)/shard_map/bcp,bpr->cr/dot_general | solution.py:80
  9.1 0.7 all-gather.3.cloned.1.call-update
  9.8 46.2 %all-reduce.2.cloned.1.call-done = bf16[1,256,256]{2,1,0:T(8,128)(2,1)} async-done(((bf16[1,256,256]{2,1,0:T(8,128)(2,1)}), bf16[1,256,256]{2,1,0:T(8,128)(2,1)}) %all-reduce.2.cloned.1.call-update) | async-done | bytes 131088 | tf_op jit(solution)/shard_map/psum | solution.py:84
  56.0 46.2 %all-gather.3.cloned.1.call-done = bf16[48,128,256]{2,1,0:T(8,128)(2,1)} async-done(((bf16[12,128,256]{2,1,0:T(8,128)(2,1)}), bf16[48,128,256]{2,1,0:T(8,128)(2,1)}) %all-gather.3.cloned.1.call-update) | async-done | bytes 3145744 | tf_op jit(solution)/shard_map/all_gather | solution.py:72
  102.2 5.1 %collective-permute-start = (bf16[48,128,256]{2,1,0:T(8,128)(2,1)}, bf16[48,128,256]{2,1,0:T(8,128)(2,1)}, u32[]{:S(2)}, u32[]{:S(2)}) collective-permute-start(bf16[48,128,256]{2,1,0:T(8,128)(2,1)} %all-gather.3.cloned.1.call-done), channel_id=1, source_target_pairs={{0,4},{4,8},{8,12},{12,16},{16,20},{20,24},{24,28},{28,32},{32,36}... | collective-permute-start | bytes 9437192 | tf_op jit(solution)/shard_map/ppermute | solution.py:15
  107.3 1.9 collective-permute-start.1
  109.3 0.7 fusion.15
  110.0 2.9 %gather_fusion.1 = bf16[32,256,256]{2,1,0:T(8,128)(2,1)} fusion(bf16[8,256,256]{2,1,0:T(8,128)(2,1)S(1)} %copy-done, s32[1024]{0:T(1024)S(1)} %pad_clamp_fusion.3), kind=kCustom, calls=%fused_computation.1 | custom fusion | bytes 8388736 | tf_op jit(solution)/shard_map/gather | solution.py:48
  112.9 0.6 gather_fusion.3
  113.6 0.1 reshape.140
  113.8 33.0 %collective-permute-done = bf16[48,128,256]{2,1,0:T(8,128)(2,1)} collective-permute-done((bf16[48,128,256]{2,1,0:T(8,128)(2,1)}, bf16[48,128,256]{2,1,0:T(8,128)(2,1)}, u32[]{:S(2)}, u32[]{:S(2)}) %collective-permute-start) | collective-permute-done | bytes 3145760 | tf_op jit(solution)/shard_map/ppermute | solution.py:15
  146.8 7.7 %collective-permute-done.1 = bf16[48,128,256]{2,1,0:T(8,128)(2,1)} collective-permute-done((bf16[48,128,256]{2,1,0:T(8,128)(2,1)}, bf16[48,128,256]{2,1,0:T(8,128)(2,1)}, u32[]{:S(2)}, u32[]{:S(2)}) %collective-permute-start.1) | collective-permute-done | bytes 3145760 | tf_op jit(solution)/shard_map/ppermute | solution.py:17
  154.5 8.4 %pad_maximum_fusion = bf16[144,128,256]{2,1,0:T(8,128)(2,1)} fusion(bf16[48,128,256]{2,1,0:T(8,128)(2,1)} %collective-permute-done.1, bf16[48,128,256]{2,1,0:T(8,128)(2,1)} %all-gather.3.cloned.1.call-done, bf16[48,128,256]{2,1,0:T(8,128)(2,1)} %collective-permute-done), kind=kLoop, calls=%fused_computation.7 | loop fusion | flops 9437184 | bytes 18874368 | tf_op jit(solution)/shard_map/concatenate | solution.py:13
  162.9 12.0 %gather_fusion = bf16[192,128,256]{2,1,0:T(8,128)(2,1)} fusion(bf16[144,128,256]{2,1,0:T(8,128)(2,1)} %pad_maximum_fusion, s32[1024]{0:T(1024)S(1)} %pad_clamp_fusion.4), kind=kCustom, calls=%fused_computation | custom fusion | bytes 25166592 | tf_op jit(solution)/shard_map/gather | solution.py:74
  174.9 16.8 %copy.16 = bf16[12,16,128,256]{2,3,1,0:T(8,128)(2,1)} copy(bf16[12,16,128,256]{3,2,1,0:T(8,128)(2,1)} %bitcast.66) | data formatting | bytes 25165824 | tf_op jit(solution)/shard_map/gather | solution.py:74
  191.6 6.1 %gather_fusion.2 = bf16[32,256,256]{2,1,0:T(8,128)(2,1)} fusion(bf16[64,256,256]{2,1,0:T(8,128)(2,1)} %all-gather.5.cloned.1.call-done, s32[1024]{0:T(1024)S(1)} %pad_clamp_fusion.2), kind=kCustom, calls=%fused_computation.2 | custom fusion | bytes 8388736 | tf_op jit(solution)/shard_map/gather | solution.py:49
  197.8 5.3 %convolution_bitcast_fusion.1 = f32[256,256]{0,1:T(8,128)S(1)} fusion(bf16[32,256,256]{2,1,0:T(8,128)(2,1)} %gather_fusion.1, bf16[32,256,256]{2,1,0:T(8,128)(2,1)} %gather_fusion.2), kind=kOutput, calls=%fused_computation.14 | convolution fusion | flops 1073741824 | bytes 8650752 | tf_op jit(solution)/shard_map/kcd,kdr->cr/dot_general | solution.py:46
  203.1 0.5 copy-done.2
  203.6 3.7 %fusion.5 = bf16[8,256,256]{1,2,0:T(8,128)(2,1)S(1)} fusion(bf16[8,8,256,256]{3,2,1,0:T(8,128)(2,1)S(1)} %bitcast.67, bf16[8,256,256]{2,1,0:T(8,128)(2,1)} %param.19), kind=kOutput, calls=%fused_computation.11 | convolution fusion | flops 2148007936 | bytes 10485760 | tf_op jit(solution)/shard_map/get,kgtv->kev/dot_general | solution.py:37
  207.3 0.6 gather_fusion.4
  207.9 1.7 fusion.9
  209.6 1.5 fusion.20
  211.2 11.1 %bitcast_add_fusion = f32[12,128,256]{1,2,0:T(8,128)} fusion(f32[256,12,128]{2,0,1:T(8,128)S(1)} %fusion.20, bf16[12,16,128,128]{3,2,1,0:T(8,128)(2,1)} %param.14, bf16[12,16,128,256]{2,3,1,0:T(8,128)(2,1)} %copy.16, bf16[12,16]{1,0:T(8,128)(2,1)S(1)} %fusion.14), kind=kOutput, calls=%fused_computation.10 | convolution fusion | flops 1617297408 | bytes 22020480 | tf_op jit(solution)/shard_map/bkpq,bkqr->bpr/dot_general | solution.py:79
  222.3 3.0 %copy.17 = f32[12,128,256]{2,1,0:T(8,128)} copy(f32[12,128,256]{1,2,0:T(8,128)} %bitcast_add_fusion) | data formatting | bytes 3145728 | tf_op jit(solution)/shard_map/add | solution.py:98
  (31 shorter events, 0.3 us)
Async XLA Ops:
  6.5 103.4 %copy-start = (bf16[8,256,256]{2,1,0:T(8,128)(2,1)S(1)}, bf16[8,256,256]{2,1,0:T(8,128)(2,1)}, u32[]{:S(2)}) copy-start(bf16[8,256,256]{2,1,0:T(8,128)(2,1)} %param.21) | copy-start | bytes 3145732
  6.5 49.5 %all-reduce.2.cloned.1.call-start = ((), (), s32[]{:S(2)}) async-start(), calls=%async_computation.1 | async-start | bytes 262144 | tf_op jit(solution)/shard_map/psum | solution.py:84
  9.1 93.2 %all-gather.3.cloned.1.call-start = ((), (), s32[]{:S(2)}) async-start(), calls=%async_computation | async-start | bytes 3932160 | tf_op jit(solution)/shard_map/all_gather | solution.py:72
  9.8 181.8 %all-gather.5.cloned.1.call-start = ((), (), s32[]{:S(2)}) async-start(), calls=%async_computation.2 | async-start | bytes 8519680 | tf_op jit(solution)/shard_map/all_gather | solution.py:85
  102.2 44.5 %collective-permute-start = (bf16[48,128,256]{2,1,0:T(8,128)(2,1)}, bf16[48,128,256]{2,1,0:T(8,128)(2,1)}, u32[]{:S(2)}, u32[]{:S(2)}) collective-permute-start(bf16[48,128,256]{2,1,0:T(8,128)(2,1)} %all-gather.3.cloned.1.call-done), channel_id=1, source_target_pairs={{0,4},{4,8},{8,12},{12,16},{16,20},{20,24},{24,28},{28,32},{32,36}... | collective-permute-start | bytes 9437192 | tf_op jit(solution)/shard_map/ppermute | solution.py:15
  107.3 47.1 %collective-permute-start.1 = (bf16[48,128,256]{2,1,0:T(8,128)(2,1)}, bf16[48,128,256]{2,1,0:T(8,128)(2,1)}, u32[]{:S(2)}, u32[]{:S(2)}) collective-permute-start(bf16[48,128,256]{2,1,0:T(8,128)(2,1)} %all-gather.3.cloned.1.call-done), channel_id=1, source_target_pairs={{4,0},{8,4},{12,8},{16,12},{20,16},{24,20},{28,24},{32,28},{36,32}... | collective-permute-start | bytes 9437192 | tf_op jit(solution)/shard_map/ppermute | solution.py:17
  110.0 2.9 %copy-start.5 = (s32[1,8]{1,0:T(1,128)S(1)}, s32[1,8]{1,0:T(1,128)}, u32[]{:S(2)}) copy-start(s32[1,8]{1,0:T(1,128)} %param.25) | copy-start | bytes 100
  110.0 3.6 %copy-start.3 = (s32[12,16]{1,0:T(8,128)S(1)}, s32[12,16]{1,0:T(8,128)}, u32[]{:S(2)}) copy-start(s32[12,16]{1,0:T(8,128)} %param.15) | copy-start | bytes 2308
  110.0 3.6 %copy-start.6 = (s32[1,32]{1,0:T(1,128)S(1)}, s32[1,32]{1,0:T(1,128)}, u32[]{:S(2)}) copy-start(s32[1,32]{1,0:T(1,128)} %param.22) | copy-start | bytes 388
  110.0 3.7 %copy-start.7 = (s32[1,8]{1,0:T(1,128)S(1)}, s32[1,8]{1,0:T(1,128)}, u32[]{:S(2)}) copy-start(s32[1,8]{1,0:T(1,128)} %param.24) | copy-start | bytes 100
  110.0 3.7 %copy-start.4 = (s32[12]{0:T(128)S(1)}, s32[12]{0:T(128)}, u32[]{:S(2)}) copy-start(s32[12]{0:T(128)} %param.16) | copy-start | bytes 148
  197.8 5.8 %copy-start.2 = (bf16[64,256,256]{2,1,0:T(8,128)(2,1)S(1)}, bf16[64,256,256]{2,1,0:T(8,128)(2,1)}, u32[]{:S(2)}) copy-start(bf16[64,256,256]{2,1,0:T(8,128)(2,1)} %all-gather.5.cloned.1.call-done) | copy-start | bytes 25165828
  211.2 14.2 %copy-start.1 = (bf16[8,256,256]{2,1,0:T(8,128)(2,1)S(1)}, bf16[8,256,256]{2,1,0:T(8,128)(2,1)}, u32[]{:S(2)}) copy-start(bf16[8,256,256]{2,1,0:T(8,128)(2,1)} %param.21) | copy-start | bytes 3145732
Sparse Core Ops, SparseCore 0:
  9.6 46.3 all-reduce.1
  57.8 44.3 all-gather.2
  105.0 81.0 all-gather.4
where the time goes:
time: 233 us; the launch traced here: 232 us
  waiting for transfers between devices  134 us (58%)
  local copies, waits for them, and re-layouts  42.6 us (18%)
  matrix products  25.9 us (11%)
  between operations  13.3 us (6%)
  other arithmetic  9.2 us (4%)
  starting transfers between devices  7.09 us (3%)
    all_gather x1, waiting for transfers between devices, on_device(): subtree = lax.all_gather(charges, 'level', axis=0, tiled=True)  46.2 us
    psum x1, waiting for transfers between devices, on_device(): moment = lax.psum(partial_moment.astype(jnp.bfloat16), 'level')  46.2 us
    ppermute x1, waiting for transfers between devices, extended_2(): lax.ppermute(tail, axis, [(i, (i + 1) % count) for i in range(ends)])  33 us
    gather x2, local copies, waits for them, and re-layouts, on_device(): picked = extended[near_source]  28.7 us
    dot_general x1, matrix products, on_device(): jnp.einsum('bkpq,bkqr->bpr', near_mat, picked, preferred_element_type=jnp...  11.1 us
    concatenate x1, other arithmetic, extended_2(): jnp.concatenate([lax.ppermute(tail, axis, [(i, (i + 1) % count) for i in...  8.42 us
    ppermute x1, waiting for transfers between devices, extended_2(): lax.ppermute(head, axis, [((i + 1) % count, i) for i in range(ends)])  7.72 us
    gather x1, local copies, waits for them, and re-layouts, top_tree(): every[subtree_interaction_list[0]]  6.13 us
  transfers between devices with their start and end apart: 5, of which 4 were waited for; matrix products, arithmetic and copies ran while one was open for 18% of the time, Pallas kernels for 0%

commit v1 on v0

v1 whole, which is shorter than its diff:
```python
import jax
import jax.numpy as jnp
from jax import lax
from jax.experimental import pallas as pl
from jax.experimental.pallas import tpu as pltpu
from jax.sharding import PartitionSpec as P


BOTH = ("leaf", "level")
NT = (((1,), (1,)), ((), ()))
F32 = jnp.float32
BF16 = jnp.bfloat16


def dot(a, b):
    return jnp.dot(a, b, preferred_element_type=F32)


def dot_nt(a, b):
    return lax.dot_general(a, b, NT, preferred_element_type=F32)


def moment_kernel(charges, maps, cells, ops, parents, parent_ops, out, row):
    blocks = charges.shape[0]
    total = None
    for b in range(0, blocks, 2):
        left = jnp.concatenate([maps[b], maps[b + 1]], axis=1)
        right = jnp.concatenate([charges[b], charges[b + 1]], axis=0)
        part = dot(left, right)
        total = part if total is None else total + part
    total = total.astype(BF16)
    row[...] = jnp.zeros_like(row)
    row[0:1, 0:32] = ((cells[...] & 7) * 8 + (cells[...] >> 3)).astype(F32)
    row[0:1, 32:64] = ops[...].astype(F32)
    row[0:1, 64:72] = parents[...].astype(F32)
    row[0:1, 72:80] = parent_ops[...].astype(F32)
    rows, cols = iota((1024, 512), 0), iota((1024, 512), 1)
    spread = jnp.where(rows == (cols & 255) * 4 + (cols >> 8), 1.0, 0.0).astype(BF16)
    parts = dot_nt(spread, jnp.concatenate([total[0:128], total[128:256]], axis=1))
    lists = jnp.broadcast_to(row[0:1, :], (1024, 128))
    out[...] = jnp.where((iota((1024, 128), 0) & 3) == 2, lists, parts).astype(BF16)


def iota(shape, dim):
    return lax.broadcasted_iota(jnp.int32, shape, dim)


def split(x):
    high = x.astype(BF16)
    return high, (x - high.astype(F32)).astype(BF16)


def far_kernel(received, upward_hbm, transfer_hbm, shift_hbm, out, upward, transfer, shift, sems):
    pairs = ((upward_hbm, upward), (transfer_hbm, transfer), (shift_hbm, shift))
    copies = [pltpu.make_async_copy(a, b, sems.at[n]) for n, (a, b) in enumerate(pairs)]
    for copy in copies:
        copy.start()
    rows, cols = iota((64, 1024), 0), iota((64, 1024), 1)
    cell = (rows & 7) * 8 + (rows >> 3)
    chosen = []
    for j in range(2):
        chosen.append(jnp.where(((cols >> 4) == cell) & ((cols & 3) == j), 1.0, 0.0))
    chosen.append(jnp.where(cols == cell * 16 + 2, 1.0, 0.0))
    gathered = dot(jnp.concatenate(chosen, axis=0).astype(BF16), received[...])
    moments = jnp.concatenate([gathered[0:64], gathered[64:128]], axis=1).astype(BF16)
    lists = gathered[128:192]
    lane = iota((64, 128), 1).astype(F32)

    codes = lists[:, 32:64] * 64.0 + lists[:, 0:32]
    counts = [jnp.zeros((64, 128), F32) for _ in range(4)]
    for k in range(32):
        code = jnp.broadcast_to(codes[:, k : k + 1], (64, 128)) - lane
        for g in range(4):
            counts[g] = counts[g] + jnp.where(code == 128.0 * g, 1.0, 0.0)
    parent_codes = lists[:, 72:80] * 8.0 + lists[:, 64:72]
    parent_counts = jnp.zeros((64, 128), F32)
    for k in range(8):
        code = jnp.broadcast_to(parent_codes[:, k : k + 1], (64, 128))
        parent_counts = parent_counts + jnp.where(code == lane, 1.0, 0.0)

    first = lane < 64.0
    picks = []
    for g in range(4):
        picks.append(jnp.where(first, counts[g], 0.0))
        picks.append(jnp.where(first, 0.0, counts[g]))
    picks = jnp.concatenate(picks, axis=0).astype(BF16)
    sums = dot(picks, jnp.concatenate([moments, moments], axis=0))
    high, low = split(sums)

    for copy in copies:
        copy.wait()
    wide = moments.astype(F32)
    upper = jnp.zeros((8, 256), F32)
    for i in range(8):
        upper = upper + dot_nt(wide[8 * i : 8 * i + 8].astype(BF16), upward[i])
    upper = upper.astype(BF16)

    far = jnp.zeros((64, 256), F32)
    moved = []
    for o in range(8):
        both = jnp.concatenate([high[64 * o : 64 * o + 64], low[64 * o : 64 * o + 64]], axis=0)
        part = dot_nt(both, transfer[o])
        far = far + part[0:64] + part[64:128]
        moved.append(dot_nt(upper, transfer[o]))
    moved_high, moved_low = split(jnp.concatenate(moved, axis=0))
    weights = parent_counts[:, 0:64].astype(BF16)
    coarse = dot(weights, moved_high) + dot(weights, moved_low)
    coarse = coarse.astype(BF16).astype(F32)
    down = [dot_nt(coarse[8 * j : 8 * j + 8].astype(BF16), shift[j]) for j in range(8)]
    local = (far + jnp.concatenate(down, axis=0)).astype(BF16)

    rows, cols = iota((512, 128), 0), iota((512, 128), 1)
    cell = (cols & 7) * 8 + ((cols >> 3) & 7)
    spread = jnp.where(((rows >> 3) == cell) & ((rows & 1) == (cols >> 6)), 1.0, 0.0).astype(BF16)
    out[...] = dot(spread, jnp.concatenate([local[:, 0:128], local[:, 128:256]], axis=0)).astype(BF16)


def panel_kernel(sources, counts, *refs):
    buffers, (mats, evals, local, out, window, turned, sems) = refs[:-7], refs[-7:]
    b = pl.program_id(0)

    @pl.when(b == 0)
    def _():
        copies = []
        for n, buffer in enumerate(buffers):
            copies.append(pltpu.make_async_copy(buffer, window.at[pl.ds(n * 12, 12)], sems.at[n]))
        for copy in copies:
            copy.start()
        rows, cols = iota((512, 512), 0), iota((512, 512), 1)
        order = jnp.where(rows == (cols & 255) * 2 + (cols >> 8), 1.0, 0.0).astype(BF16)
        both = lax.dot_general(local[...], order, (((0,), (0,)), ((), ())), preferred_element_type=F32)
        turned[0:128, :] = both[:, 0:256].astype(BF16)
        turned[128:256, :] = both[:, 256:512].astype(BF16)
        for copy in copies:
            copy.wait()

    count = counts[b]

    def pair(k):
        left = jnp.concatenate(
            [
                jnp.where(k < count, mats[0, k], 0).astype(BF16),
                jnp.where(k + 1 < count, mats[0, k + 1], 0).astype(BF16),
            ],
            axis=1,
        )
        right = jnp.concatenate([window[sources[b * 16 + k]], window[sources[b * 16 + k + 1]]], axis=0)
        return dot(left, right)

    total = dot(evals[0], turned[...])
    for k in range(0, 8, 2):
        total = total + pair(k)
    out[0] = total

    @pl.when(count > 8)
    def _():
        more = pair(8)
        for k in range(10, 16, 2):
            more = more + pair(k)
        out[0] = out[0] + more


def call_moment(*args):
    return pl.pallas_call(
        moment_kernel,
        out_shape=jax.ShapeDtypeStruct((1024, 128), BF16),
        scratch_shapes=[pltpu.VMEM((8, 128), F32)],
        name="moment",
    )(*args)


def call_far(received, *weights):
    return pl.pallas_call(
        far_kernel,
        out_shape=jax.ShapeDtypeStruct((512, 128), BF16),
        in_specs=[pl.BlockSpec(memory_space=pltpu.VMEM)] + [pl.BlockSpec(memory_space=pltpu.HBM)] * 3,
        scratch_shapes=[pltpu.VMEM(w.shape, BF16) for w in weights] + [pltpu.SemaphoreType.DMA((3,))],
        compiler_params=pltpu.CompilerParams(vmem_limit_bytes=60 << 20),
        name="far",
    )(received, *weights)


def call_panel(sources, counts, buffers, mats, evals, local):
    blocks = mats.shape[0]
    total = sum(x.shape[0] for x in buffers)
    return pl.pallas_call(
        panel_kernel,
        out_shape=jax.ShapeDtypeStruct((blocks, 128, 256), F32),
        grid_spec=pltpu.PrefetchScalarGridSpec(
            num_scalar_prefetch=2,
            grid=(blocks,),
            in_specs=[pl.BlockSpec(memory_space=pltpu.HBM)] * len(buffers)
            + [
                pl.BlockSpec((1, 16, 128, 128), lambda b, *_: (b, 0, 0, 0)),
                pl.BlockSpec((1, 128, 256), lambda b, *_: (b, 0, 0)),
                pl.BlockSpec((512, 128), lambda b, *_: (0, 0)),
            ],
            out_specs=pl.BlockSpec((1, 128, 256), lambda b, *_: (b, 0, 0)),
            scratch_shapes=[
                pltpu.VMEM((total, 128, 256), BF16),
                pltpu.VMEM((256, 256), BF16),
                pltpu.SemaphoreType.DMA((len(buffers),)),
            ],
        ),
        compiler_params=pltpu.CompilerParams(vmem_limit_bytes=56 << 20),
        name="panel",
    )(sources, counts, *buffers, mats, evals, local)


def flat(pairs):
    return [(a * 4 + b, c * 4 + d) for (a, b), (c, d) in pairs]


def outer(leaf):
    return leaf + 1 if leaf % 2 else leaf - 1


def outer_pairs(leaves, turn):
    return flat(
        [
            ((leaf, y), (outer(leaf), (y + turn) % 4))
            for leaf in range(leaves)
            for y in range(4)
            if 0 <= outer(leaf) < leaves
        ]
    )


def inner_pairs(leaves):
    return flat([((leaf, y), (leaf ^ 1, y)) for leaf in range(leaves) for y in range(4)])


def on_device(
    charges,
    near_mat,
    near_source,
    near_count,
    moment_map,
    local_eval,
    upward_child_translation,
    shift_down,
    transfer_ops,
    subtree_interaction_list,
    subtree_interaction_operators,
    parent_list,
    parent_ops,
):
    leaves = lax.axis_size("leaf")
    leaf, level = lax.axis_index("leaf"), lax.axis_index("level")
    ring = [(i, (i + 1) % 4) for i in range(4)]
    back = [((i + 1) % 4, i) for i in range(4)]
    inner = inner_pairs(leaves)

    below = lax.ppermute(charges, "level", ring)
    above = lax.ppermute(charges, "level", back)
    outer_own = lax.ppermute(charges, BOTH, outer_pairs(leaves, 0))
    inner_own = lax.ppermute(charges, BOTH, inner)

    lists = (subtree_interaction_list, subtree_interaction_operators, parent_list, parent_ops)
    message = call_moment(charges, moment_map, *lists)
    received = lax.all_to_all(message.reshape(256, 4, 128), BOTH, 0, 0, tiled=True).reshape(1024, 128)

    received, below, above, outer_own = lax.optimization_barrier((received, below, above, outer_own))
    outer_below = lax.ppermute(below, BOTH, outer_pairs(leaves, 0))
    outer_above = lax.ppermute(above, BOTH, outer_pairs(leaves, 0))
    far_own = lax.ppermute(below, "level", ring)
    outer_far = lax.ppermute(above, BOTH, outer_pairs(leaves, -1))
    inner_below = lax.ppermute(below, BOTH, inner)
    inner_above = lax.ppermute(above, BOTH, inner)

    columns = call_far(received, upward_child_translation, transfer_ops, shift_down)
    local = lax.all_to_all(columns.reshape(256, 2, 128), BOTH, 0, 0, tiled=True).reshape(512, 128)

    local, far_own = lax.optimization_barrier((local, far_own))
    inner_far = lax.ppermute(far_own, BOTH, inner)

    buffers = [
        charges, above, far_own, below,
        inner_own, inner_above, inner_far, inner_below,
        outer_own, outer_above, outer_far, outer_below,
    ]
    subtree, place = near_source // 48, near_source % 48
    turn = (place // 12 - level) & 3
    odd = leaf & 1
    group = jnp.where(subtree == 1, 0, jnp.where((subtree == 0) == (odd == 1), 1, 2))
    sources = (group * 48 + turn * 12 + place % 12).reshape(-1)
    return call_panel(sources, near_count, buffers, near_mat, local_eval, local)


def solution(mesh):
    placed = (
        P(("leaf", "level"), None, None),
        P(("leaf", "level"), None, None, None),
        P(("leaf", "level"), None),
        P(("leaf", "level")),
        P(("leaf", "level"), None, None),
        P(("leaf", "level"), None, None),
        P(),
        P(),
        P(),
        P("leaf", None),
        P("leaf", None),
        P("leaf", None),
        P("leaf", None),
    )
    return jax.shard_map(
        on_device,
        mesh=mesh,
        in_specs=placed,
        out_specs=P(("leaf", "level"), None, None),
        check_vma=False,
    )
```

time: 233 us -> 97.1 us (0.42)
  waiting for transfers between devices: 134 us -> 14.1 us
  local copies, waits for them, and re-layouts: 42.6 us -> 0.67 us
  starting transfers between devices: 7.09 us -> 33.8 us
  matrix products: 25.9 us -> 0 us
  Pallas kernels: 0 us -> 23.8 us
  blocking collectives: 0 us -> 22.8 us
  between operations: 13.3 us -> 0.18 us
  other arithmetic: 9.2 us -> 0.73 us
    all_gather x2 -> x0, waiting for transfers between devices: 46.2 us -> none  [the longest x1 46.2 us: on_device(): subtree = lax.all_gather(charges, 'level', axis=0, tiled=True)]
    psum x1 -> x0, waiting for transfers between devices: 46.2 us -> none  [on_device(): moment = lax.psum(partial_moment.astype(jnp.bfloat16), 'level')]
    gather x6 -> x0, local copies, waits for them, and re-layouts: 38.9 us -> none  [the longest x2 28.7 us: on_device(): picked = extended[near_source]]
    ppermute x2 -> x11, waiting for transfers between devices: 40.7 us -> 14.1 us  [the longest x1 8.42 us: on_device(): outer_below = lax.ppermute(below, BOTH, outer_pairs(leaves, 0))]
    dot_general x6 -> x0, matrix products: 25.9 us -> none  [the longest x1 11.1 us: on_device(): jnp.einsum('bkpq,bkqr->bpr', near_mat, picked, preferred_element_type=jnp...]
    pallas_call x0 -> x3, Pallas kernels: none -> 23.8 us  [the longest x1 15.2 us: call_panel(): pl.pallas_call(panel_kernel, out_shape=jax.ShapeDtypeStruct((blocks, 128,...]
    all_to_all x0 -> x1, blocking collectives: none -> 22.8 us  [on_device(): lax.all_to_all(message.reshape(256, 4, 128), BOTH, 0, 0, tiled=True)]
    ppermute x2 -> x11, starting transfers between devices: 7.01 us -> 24.6 us  [the longest x1 5.63 us: on_device(): outer_far = lax.ppermute(above, BOTH, outer_pairs(leaves, -1))]
  transfers between devices with their start and end apart: 5 -> 12, of which waited for: 4 -> 2; matrix products, arithmetic and copies ran while one was open for 18% -> 1% of each run, Pallas kernels for 0% -> 9%
where the time goes in v1:
time: 97.1 us; the launch traced here: 96.1 us
  starting transfers between devices  33.8 us (35%)
  Pallas kernels  23.8 us (25%)
  blocking collectives  22.8 us (23%)
  waiting for transfers between devices  14.1 us (15%)
    all_to_all x1, blocking collectives, on_device(): lax.all_to_all(message.reshape(256, 4, 128), BOTH, 0, 0, tiled=True)  22.8 us
    pallas_call x1, Pallas kernels, call_panel(): pl.pallas_call(panel_kernel, out_shape=jax.ShapeDtypeStruct((blocks, 128,...  15.2 us
    all_to_all x1, starting transfers between devices, on_device(): lax.all_to_all(columns.reshape(256, 2, 128), BOTH, 0, 0, tiled=True)  9.24 us
    ppermute x1, waiting for transfers between devices, on_device(): outer_below = lax.ppermute(below, BOTH, outer_pairs(leaves, 0))  8.42 us
    ppermute x1, waiting for transfers between devices, on_device(): outer_above = lax.ppermute(above, BOTH, outer_pairs(leaves, 0))  5.7 us
    ppermute x1, starting transfers between devices, on_device(): outer_far = lax.ppermute(above, BOTH, outer_pairs(leaves, -1))  5.63 us
    pallas_call x1, Pallas kernels, call_far(): pl.pallas_call(far_kernel, out_shape=jax.ShapeDtypeStruct((512, 128), BF1...  5.37 us
    ppermute x1, starting transfers between devices, on_device(): outer_own = lax.ppermute(charges, BOTH, outer_pairs(leaves, 0))  5.22 us
  transfers between devices with their start and end apart: 12, of which 2 were waited for; matrix products, arithmetic and copies ran while one was open for 1% of the time, Pallas kernels for 9%

profile of v1, /device:TPU:103, one launch (start us, length us, event | category | flops | bytes accessed | tf_op | source)
XLA Modules:
  0.0 96.1 jit_solution(6730960184747577203)
XLA Ops:
  0.0 5.2 %collective-permute-start.2 = (bf16[12,128,256]{2,1,0:T(8,128)(2,1)}, bf16[12,128,256]{2,1,0:T(8,128)(2,1)S(1)}, u32[]{:S(2)}, u32[]{:S(2)}) collective-permute-start(bf16[12,128,256]{2,1,0:T(8,128)(2,1)} %refs_0_.1), channel_id=1, source_target_pairs={{4,8},{5,9},{6,10},{7,11},{8,4},{9,5},{10,6},{11,7},{12,16},{13,17... | collective-permute-start | bytes 2359304 | tf_op jit(solution)/shard_map/ppermute | solution.py:256
  5.2 2.8 %collective-permute-start.1 = (bf16[12,128,256]{2,1,0:T(8,128)(2,1)}, bf16[12,128,256]{2,1,0:T(8,128)(2,1)S(1)}, u32[]{:S(2)}, u32[]{:S(2)}) collective-permute-start(bf16[12,128,256]{2,1,0:T(8,128)(2,1)} %refs_0_.1), channel_id=1, source_target_pairs={{1,0},{2,1},{3,2},{0,3},{5,4},{6,5},{7,6},{4,7},{9,8},{10,9},{11,1... | collective-permute-start | bytes 2359304 | tf_op jit(solution)/shard_map/ppermute | solution.py:255
  8.0 0.0 collective-permute-start
  8.0 3.2 %moment.1 = bf16[1024,128]{1,0:T(8,128)(2,1)} custom-call(bf16[12,128,256]{2,1,0:T(8,128)(2,1)} %refs_0_.1, bf16[12,256,128]{2,1,0:T(8,128)(2,1)} %maps.1, s32[1,32]{1,0:T(1,128)} %cells.1, s32[1,32]{1,0:T(1,128)} %ops.1, s32[1,8]{1,0:T(1,128)} %parents.1, s32[1,8]{1,0:T(1,128)} %parent_ops.1), custom_call_target="tpu_custom_call" | custom-call | tf_op jit(solution)/shard_map/moment/pallas_call | solution.py:164
  11.3 22.8 %all_to_all.10 = bf16[256,4,128]{2,1,0:T(4,128)(2,1)} all-to-all(bf16[256,4,128]{2,1,0:T(4,128)(2,1)} %bitcast.5), channel_id=1, replica_groups=mesh['leaf'=64,'level'=4] {'leaf','level'}, dimensions={0} | all-to-all | bytes 524288 | tf_op jit(solution)/shard_map/all_to_all | solution.py:261
  34.1 0.0 collective-permute-done.2.refs_8_
  34.1 0.0 collective-permute-done.1.refs_1_
  34.1 0.0 collective-permute-done.refs_3_
  34.1 0.3 collective-permute-start.3
  34.4 1.0 %collective-permute-start.4 = (bf16[12,128,256]{2,1,0:T(8,128)(2,1)}, bf16[12,128,256]{2,1,0:T(8,128)(2,1)}, u32[]{:S(2)}, u32[]{:S(2)}) collective-permute-start(bf16[12,128,256]{2,1,0:T(8,128)(2,1)} %refs_0_.1), channel_id=1, source_target_pairs={{0,4},{1,5},{2,6},{3,7},{4,0},{5,1},{6,2},{7,3},{8,12},{9,13},{10,... | collective-permute-start | bytes 2359304 | tf_op jit(solution)/shard_map/ppermute | solution.py:257
  35.5 5.6 %collective-permute-start.9 = (bf16[12,128,256]{2,1,0:T(8,128)(2,1)S(1)}, bf16[12,128,256]{2,1,0:T(8,128)(2,1)}, u32[]{:S(2)}, u32[]{:S(2)}) collective-permute-start(bf16[12,128,256]{2,1,0:T(8,128)(2,1)S(1)} %collective-permute-done.1.refs_1_), channel_id=1, source_target_pairs={{4,11},{5,8},{6,9},{7,10},{8,7},{9,4},{10,5},{11,6},{12,19},{13,16... | collective-permute-start | bytes 2359304 | tf_op jit(solution)/shard_map/ppermute | solution.py:267
  41.1 5.4 %far.1 = bf16[512,128]{1,0:T(8,128)(2,1)} custom-call(bf16[1024,128]{1,0:T(8,128)(2,1)} %bitcast.4, bf16[8,256,256]{2,1,0:T(8,128)(2,1)} %upward_hbm.1, bf16[8,256,256]{2,1,0:T(8,128)(2,1)} %transfer_hbm.1, bf16[8,256,256]{2,1,0:T(8,128)(2,1)} %shift_hbm.1), custom_call_target="tpu_custom_call" | custom-call | tf_op jit(solution)/shard_map/far/pallas_call | solution.py:173
  46.5 9.2 %all-to-all-start.1 = ((bf16[256,2,128]{2,1,0:T(2,128)(2,1)}), bf16[256,2,128]{2,1,0:T(2,128)(2,1)S(1)}, u32[]{:S(2)}, u32[]{:S(2)}) async-start(bf16[256,2,128]{2,1,0:T(2,128)(2,1)} %bitcast.7), calls=%async_computation.1 | async-start | bytes 262144 | tf_op jit(solution)/shard_map/all_to_all | solution.py:272
  55.7 4.8 %collective-permute-start.8 = (bf16[12,128,256]{2,1,0:T(8,128)(2,1)S(1)}, bf16[12,128,256]{2,1,0:T(8,128)(2,1)}, u32[]{:S(2)}, u32[]{:S(2)}) collective-permute-start(bf16[12,128,256]{2,1,0:T(8,128)(2,1)S(1)} %collective-permute-done.1.refs_1_), channel_id=1, source_target_pairs={{4,8},{5,9},{6,10},{7,11},{8,4},{9,5},{10,6},{11,7},{12,16},{13,17... | collective-permute-start | bytes 2359304 | tf_op jit(solution)/shard_map/ppermute | solution.py:265
  60.5 0.1 collective-permute-start.5
  60.6 4.1 %collective-permute-start.10 = (bf16[12,128,256]{2,1,0:T(8,128)(2,1)S(1)}, bf16[12,128,256]{2,1,0:T(8,128)(2,1)}, u32[]{:S(2)}, u32[]{:S(2)}) collective-permute-start(bf16[12,128,256]{2,1,0:T(8,128)(2,1)S(1)} %collective-permute-done.refs_3_), channel_id=1, source_target_pairs={{4,8},{5,9},{6,10},{7,11},{8,4},{9,5},{10,6},{11,7},{12,16},{13,17... | collective-permute-start | bytes 2359304 | tf_op jit(solution)/shard_map/ppermute | solution.py:264
  64.8 0.1 collective-permute-start.7
  64.9 0.5 collective-permute-start.6
  65.4 0.7 fusion.4
  66.1 0.7 reshape.15.sources
  66.8 5.7 %collective-permute-done.8.refs_9_ = bf16[12,128,256]{2,1,0:T(8,128)(2,1)} collective-permute-done((bf16[12,128,256]{2,1,0:T(8,128)(2,1)S(1)}, bf16[12,128,256]{2,1,0:T(8,128)(2,1)}, u32[]{:S(2)}, u32[]{:S(2)}) %collective-permute-start.8) | collective-permute-done | bytes 786464 | tf_op jit(solution)/shard_map/ppermute | solution.py:265
  72.5 0.0 collective-permute-done.5.refs_5_
  72.5 8.4 %collective-permute-done.10.refs_11_ = bf16[12,128,256]{2,1,0:T(8,128)(2,1)} collective-permute-done((bf16[12,128,256]{2,1,0:T(8,128)(2,1)S(1)}, bf16[12,128,256]{2,1,0:T(8,128)(2,1)}, u32[]{:S(2)}, u32[]{:S(2)}) %collective-permute-start.10) | collective-permute-done | bytes 786464 | tf_op jit(solution)/shard_map/ppermute | solution.py:264
  80.9 15.2 %panel.1 = f32[12,128,256]{2,1,0:T(8,128)} custom-call(s32[192]{0:T(256)} %reshape.15.sources, s32[12]{0:T(128)} %counts.1, bf16[12,128,256]{2,1,0:T(8,128)(2,1)} %refs_0_.1, bf16[12,128,256]{2,1,0:T(8,128)(2,1)} %copy-done.1, bf16[12,128,256]{2,1,0:T(8,128)(2,1)} %copy-done.3, bf16[12,128,256]{2,1,0:T(8,128)(2,1)} %copy-done.2, ...), custom_call_target="tpu_custom_call" | custom-call | tf_op jit(solution)/shard_map/panel/pallas_call | solution.py:186
  (16 shorter events, 0.0 us)
Async XLA Ops:
  0.0 34.1 %collective-permute-start.2 = (bf16[12,128,256]{2,1,0:T(8,128)(2,1)}, bf16[12,128,256]{2,1,0:T(8,128)(2,1)S(1)}, u32[]{:S(2)}, u32[]{:S(2)}) collective-permute-start(bf16[12,128,256]{2,1,0:T(8,128)(2,1)} %refs_0_.1), channel_id=1, source_target_pairs={{4,8},{5,9},{6,10},{7,11},{8,4},{9,5},{10,6},{11,7},{12,16},{13,17... | collective-permute-start | bytes 2359304 | tf_op jit(solution)/shard_map/ppermute | solution.py:256
  5.2 28.8 %collective-permute-start.1 = (bf16[12,128,256]{2,1,0:T(8,128)(2,1)}, bf16[12,128,256]{2,1,0:T(8,128)(2,1)S(1)}, u32[]{:S(2)}, u32[]{:S(2)}) collective-permute-start(bf16[12,128,256]{2,1,0:T(8,128)(2,1)} %refs_0_.1), channel_id=1, source_target_pairs={{1,0},{2,1},{3,2},{0,3},{5,4},{6,5},{7,6},{4,7},{9,8},{10,9},{11,1... | collective-permute-start | bytes 2359304 | tf_op jit(solution)/shard_map/ppermute | solution.py:255
  8.0 26.1 %collective-permute-start = (bf16[12,128,256]{2,1,0:T(8,128)(2,1)}, bf16[12,128,256]{2,1,0:T(8,128)(2,1)S(1)}, u32[]{:S(2)}, u32[]{:S(2)}) collective-permute-start(bf16[12,128,256]{2,1,0:T(8,128)(2,1)} %refs_0_.1), channel_id=1, source_target_pairs={{0,1},{1,2},{2,3},{3,0},{4,5},{5,6},{6,7},{7,4},{8,9},{9,10},{10,1... | collective-permute-start | bytes 2359304 | tf_op jit(solution)/shard_map/ppermute | solution.py:254
  34.1 46.8 %copy-start = (bf16[12,128,256]{2,1,0:T(8,128)(2,1)}, bf16[12,128,256]{2,1,0:T(8,128)(2,1)S(1)}, u32[]{:S(2)}) copy-start(bf16[12,128,256]{2,1,0:T(8,128)(2,1)S(1)} %collective-permute-done.2.refs_8_) | copy-start | bytes 2359300
  34.1 46.8 %copy-start.1 = (bf16[12,128,256]{2,1,0:T(8,128)(2,1)}, bf16[12,128,256]{2,1,0:T(8,128)(2,1)S(1)}, u32[]{:S(2)}) copy-start(bf16[12,128,256]{2,1,0:T(8,128)(2,1)S(1)} %collective-permute-done.1.refs_1_) | copy-start | bytes 2359300
  34.1 46.8 %copy-start.2 = (bf16[12,128,256]{2,1,0:T(8,128)(2,1)}, bf16[12,128,256]{2,1,0:T(8,128)(2,1)S(1)}, u32[]{:S(2)}) copy-start(bf16[12,128,256]{2,1,0:T(8,128)(2,1)S(1)} %collective-permute-done.refs_3_) | copy-start | bytes 2359300
  34.1 26.5 %collective-permute-start.3 = (bf16[12,128,256]{2,1,0:T(8,128)(2,1)S(1)}, bf16[12,128,256]{2,1,0:T(8,128)(2,1)S(1)}, u32[]{:S(2)}, u32[]{:S(2)}) collective-permute-start(bf16[12,128,256]{2,1,0:T(8,128)(2,1)S(1)} %collective-permute-done.refs_3_), channel_id=1, source_target_pairs={{0,1},{1,2},{2,3},{3,0},{4,5},{5,6},{6,7},{7,4},{8,9},{9,10},{10,1... | collective-permute-start | bytes 2359304 | tf_op jit(solution)/shard_map/ppermute | solution.py:266
  34.4 30.3 %collective-permute-start.4 = (bf16[12,128,256]{2,1,0:T(8,128)(2,1)}, bf16[12,128,256]{2,1,0:T(8,128)(2,1)}, u32[]{:S(2)}, u32[]{:S(2)}) collective-permute-start(bf16[12,128,256]{2,1,0:T(8,128)(2,1)} %refs_0_.1), channel_id=1, source_target_pairs={{0,4},{1,5},{2,6},{3,7},{4,0},{5,1},{6,2},{7,3},{8,12},{9,13},{10,... | collective-permute-start | bytes 2359304 | tf_op jit(solution)/shard_map/ppermute | solution.py:257
  35.5 29.4 %collective-permute-start.9 = (bf16[12,128,256]{2,1,0:T(8,128)(2,1)S(1)}, bf16[12,128,256]{2,1,0:T(8,128)(2,1)}, u32[]{:S(2)}, u32[]{:S(2)}) collective-permute-start(bf16[12,128,256]{2,1,0:T(8,128)(2,1)S(1)} %collective-permute-done.1.refs_1_), channel_id=1, source_target_pairs={{4,11},{5,8},{6,9},{7,10},{8,7},{9,4},{10,5},{11,6},{12,19},{13,16... | collective-permute-start | bytes 2359304 | tf_op jit(solution)/shard_map/ppermute | solution.py:267
  46.5 18.3 %all-to-all-start.1 = ((bf16[256,2,128]{2,1,0:T(2,128)(2,1)}), bf16[256,2,128]{2,1,0:T(2,128)(2,1)S(1)}, u32[]{:S(2)}, u32[]{:S(2)}) async-start(bf16[256,2,128]{2,1,0:T(2,128)(2,1)} %bitcast.7), calls=%async_computation.1 | async-start | bytes 262144 | tf_op jit(solution)/shard_map/all_to_all | solution.py:272
  55.7 16.7 %collective-permute-start.8 = (bf16[12,128,256]{2,1,0:T(8,128)(2,1)S(1)}, bf16[12,128,256]{2,1,0:T(8,128)(2,1)}, u32[]{:S(2)}, u32[]{:S(2)}) collective-permute-start(bf16[12,128,256]{2,1,0:T(8,128)(2,1)S(1)} %collective-permute-done.1.refs_1_), channel_id=1, source_target_pairs={{4,8},{5,9},{6,10},{7,11},{8,4},{9,5},{10,6},{11,7},{12,16},{13,17... | collective-permute-start | bytes 2359304 | tf_op jit(solution)/shard_map/ppermute | solution.py:265
  60.5 11.9 %collective-permute-start.5 = (bf16[12,128,256]{2,1,0:T(8,128)(2,1)S(1)}, bf16[12,128,256]{2,1,0:T(8,128)(2,1)}, u32[]{:S(2)}, u32[]{:S(2)}) collective-permute-start(bf16[12,128,256]{2,1,0:T(8,128)(2,1)S(1)} %collective-permute-done.1.refs_1_), channel_id=1, source_target_pairs={{0,4},{1,5},{2,6},{3,7},{4,0},{5,1},{6,2},{7,3},{8,12},{9,13},{10,... | collective-permute-start | bytes 2359304 | tf_op jit(solution)/shard_map/ppermute | solution.py:269
  60.6 20.3 %copy-start.3 = (bf16[12,128,256]{2,1,0:T(8,128)(2,1)}, bf16[12,128,256]{2,1,0:T(8,128)(2,1)S(1)}, u32[]{:S(2)}) copy-start(bf16[12,128,256]{2,1,0:T(8,128)(2,1)S(1)} %collective-permute-done.3.refs_2_) | copy-start | bytes 2359300
  60.6 20.2 %collective-permute-start.10 = (bf16[12,128,256]{2,1,0:T(8,128)(2,1)S(1)}, bf16[12,128,256]{2,1,0:T(8,128)(2,1)}, u32[]{:S(2)}, u32[]{:S(2)}) collective-permute-start(bf16[12,128,256]{2,1,0:T(8,128)(2,1)S(1)} %collective-permute-done.refs_3_), channel_id=1, source_target_pairs={{4,8},{5,9},{6,10},{7,11},{8,4},{9,5},{10,6},{11,7},{12,16},{13,17... | collective-permute-start | bytes 2359304 | tf_op jit(solution)/shard_map/ppermute | solution.py:264
  64.8 16.2 %copy-start.4 = (bf16[256,2,128]{2,1,0:T(2,128)(2,1)}, bf16[256,2,128]{2,1,0:T(2,128)(2,1)S(1)}, u32[]{:S(2)}) copy-start(bf16[256,2,128]{2,1,0:T(2,128)(2,1)S(1)} %all-to-all-done.1) | copy-start | bytes 393220
  64.8 16.1 %collective-permute-start.7 = (bf16[12,128,256]{2,1,0:T(8,128)(2,1)S(1)}, bf16[12,128,256]{2,1,0:T(8,128)(2,1)}, u32[]{:S(2)}, u32[]{:S(2)}) collective-permute-start(bf16[12,128,256]{2,1,0:T(8,128)(2,1)S(1)} %collective-permute-done.refs_3_), channel_id=1, source_target_pairs={{0,4},{1,5},{2,6},{3,7},{4,0},{5,1},{6,2},{7,3},{8,12},{9,13},{10,... | collective-permute-start | bytes 2359304 | tf_op jit(solution)/shard_map/ppermute | solution.py:268
  64.9 16.0 %collective-permute-start.6 = (bf16[12,128,256]{2,1,0:T(8,128)(2,1)S(1)}, bf16[12,128,256]{2,1,0:T(8,128)(2,1)}, u32[]{:S(2)}, u32[]{:S(2)}) collective-permute-start(bf16[12,128,256]{2,1,0:T(8,128)(2,1)S(1)} %collective-permute-done.3.refs_2_), channel_id=1, source_target_pairs={{0,4},{1,5},{2,6},{3,7},{4,0},{5,1},{6,2},{7,3},{8,12},{9,13},{10,... | collective-permute-start | bytes 2359304 | tf_op jit(solution)/shard_map/ppermute | solution.py:275

commit v2 on v1

v2 whole, which is shorter than its diff:
```python
import functools

import jax
import jax.numpy as jnp
from jax import lax
from jax.experimental import pallas as pl
from jax.experimental.pallas import tpu as pltpu
from jax.sharding import PartitionSpec as P


BOTH = ("leaf", "level")
NT = (((1,), (1,)), ((), ()))
F32 = jnp.float32
BF16 = jnp.bfloat16
GROUP = 4


def dot(a, b):
    return jnp.dot(a, b, preferred_element_type=F32)


def dot_nt(a, b):
    return lax.dot_general(a, b, NT, preferred_element_type=F32)


def moment_kernel(charges, maps, cells, ops, parents, parent_ops, *refs):
    weights, out, kept, (row, spread, sems) = refs[0:3], refs[3], refs[4:7], refs[7:]
    copies = [pltpu.make_async_copy(a, b, sems.at[n]) for n, (a, b) in enumerate(zip(weights, kept))]
    for copy in copies:
        copy.start()
    blocks = charges.shape[0]
    total = None
    for b in range(0, blocks, 2):
        left = jnp.concatenate([maps[b], maps[b + 1]], axis=1)
        right = jnp.concatenate([charges[b], charges[b + 1]], axis=0)
        part = dot(left, right)
        total = part if total is None else total + part
    turned = total.T
    row[...] = jnp.zeros_like(row)
    row[0:1, 0:32] = ((cells[...] & 7) * 8 + (cells[...] >> 3)).astype(F32)
    row[0:1, 32:64] = ops[...].astype(F32)
    row[0:1, 64:72] = parents[...].astype(F32)
    row[0:1, 72:80] = parent_ops[...].astype(F32)
    for j in range(2):
        spread[pl.ds(j, 256, stride=4), :] = turned[:, 128 * j : 128 * j + 128]
    spread[pl.ds(2, 256, stride=4), :] = jnp.broadcast_to(row[0:1, :], (256, 128))
    spread[pl.ds(3, 256, stride=4), :] = jnp.zeros((256, 128), F32)
    out[...] = spread[...].astype(BF16)
    for copy in copies:
        copy.wait()


def iota(shape, dim):
    return lax.broadcasted_iota(jnp.int32, shape, dim)


def split(x):
    high = x.astype(BF16)
    return high, (x - high.astype(F32)).astype(BF16)


def far_kernel(received, upward, transfer, shift, out):
    rows, cols = iota((64, 1024), 0), iota((64, 1024), 1)
    cell = (rows & 7) * 8 + (rows >> 3)
    chosen = []
    for j in range(2):
        chosen.append(jnp.where(((cols >> 4) == cell) & ((cols & 3) == j), 1.0, 0.0))
    chosen.append(jnp.where(cols == cell * 16 + 2, 1.0, 0.0))
    gathered = dot(jnp.concatenate(chosen, axis=0).astype(BF16), received[...])
    moments = jnp.concatenate([gathered[0:64], gathered[64:128]], axis=1).astype(BF16)
    lists = gathered[128:192]
    lane = iota((64, 128), 1).astype(F32)

    codes = lists[:, 32:64] * 64.0 + lists[:, 0:32]
    counts = [jnp.zeros((64, 128), F32) for _ in range(4)]
    for k in range(32):
        code = jnp.broadcast_to(codes[:, k : k + 1], (64, 128)) - lane
        for g in range(4):
            counts[g] = counts[g] + jnp.where(code == 128.0 * g, 1.0, 0.0)
    parent_codes = lists[:, 72:80] * 8.0 + lists[:, 64:72]
    parent_counts = jnp.zeros((64, 128), F32)
    for k in range(8):
        code = jnp.broadcast_to(parent_codes[:, k : k + 1], (64, 128))
        parent_counts = parent_counts + jnp.where(code == lane, 1.0, 0.0)

    first = lane < 64.0
    picks = []
    for g in range(4):
        picks.append(jnp.where(first, counts[g], 0.0))
        picks.append(jnp.where(first, 0.0, counts[g]))
    picks = jnp.concatenate(picks, axis=0).astype(BF16)
    sums = dot(picks, jnp.concatenate([moments, moments], axis=0))
    high, low = split(sums)

    wide = moments.astype(F32)
    upper = jnp.zeros((8, 256), F32)
    for i in range(8):
        upper = upper + dot_nt(wide[8 * i : 8 * i + 8].astype(BF16), upward[i])
    upper = upper.astype(BF16)

    far = jnp.zeros((64, 256), F32)
    moved = []
    for o in range(8):
        both = jnp.concatenate([high[64 * o : 64 * o + 64], low[64 * o : 64 * o + 64]], axis=0)
        part = dot_nt(both, transfer[o])
        far = far + part[0:64] + part[64:128]
        moved.append(dot_nt(upper, transfer[o]))
    moved_high, moved_low = split(jnp.concatenate(moved, axis=0))
    weights = parent_counts[:, 0:64].astype(BF16)
    coarse = dot(weights, moved_high) + dot(weights, moved_low)
    coarse = coarse.astype(BF16).astype(F32)
    down = [dot_nt(coarse[8 * j : 8 * j + 8].astype(BF16), shift[j]) for j in range(8)]
    local = (far + jnp.concatenate(down, axis=0)).astype(BF16)

    rows, cols = iota((512, 128), 0), iota((512, 128), 1)
    cell = (cols & 7) * 8 + ((cols >> 3) & 7)
    spread = jnp.where(((rows >> 3) == cell) & ((rows & 1) == (cols >> 6)), 1.0, 0.0).astype(BF16)
    out[...] = dot(spread, jnp.concatenate([local[:, 0:128], local[:, 128:256]], axis=0)).astype(BF16)


def gather_near(first, sources, counts, buffers, mats, window, chosen, slots, valid, blocks, sems, mat_sem):
    copies = [
        pltpu.make_async_copy(buffer, window.at[pl.ds(n * 12, 12)], sems.at[n]) for n, buffer in enumerate(buffers)
    ]
    for copy in copies:
        copy.start()
    last = first + 12 * len(buffers)

    level, odd_leaf = lax.axis_index("level"), lax.axis_index("leaf") & 1

    def place(source):
        subtree = jnp.where(source >= 48, 1, 0) + jnp.where(source >= 96, 1, 0)
        block = source - 48 * subtree
        quarter = (block * 43) >> 9
        is_inner = (subtree == 0) == (odd_leaf == 1)
        group = jnp.where(subtree == 1, 0, jnp.where(is_inner, 1, 2))
        at = group * 4 + ((quarter - level) & 3)
        at = jnp.where(at == 6, 8, jnp.where((at == 7) | (at == 8), at - 1, at))
        return at * 12 + block - 12 * quarter

    def take(b, k, n):
        source = place(sources[b, k])
        mine = (source >= first) & (source < last)

        @pl.when(mine)
        def _():
            pltpu.make_async_copy(mats.at[b, k], chosen.at[n], mat_sem).start()
            slots[n] = source - first
            valid[n] = 1
            blocks[n >> 1] = b

        return jnp.where(mine, n + 1, n)

    def take_block(b, state):
        n, used = state
        end = lax.fori_loop(0, counts[b], functools.partial(take, b), n)
        odd = (end - n) & 1

        @pl.when(odd == 1)
        def _():
            slots[end] = 0
            valid[end] = 0

        return end + odd, used + end - n

    n, used = lax.fori_loop(0, counts.shape[0], take_block, (jnp.int32(0), jnp.int32(0)))
    for extra in range(2 * GROUP):
        slots[n + extra] = 0
        valid[n + extra] = 0
        blocks[(n + extra) >> 1] = 0

    def wait(_, x):
        pltpu.make_async_copy(mats.at[0, 0], chosen.at[0], mat_sem).wait()
        return x

    lax.fori_loop(0, used, wait, 0)
    for copy in copies:
        copy.wait()
    return (n + 2 * GROUP - 1) // (2 * GROUP)


def multiply_near(steps, window, chosen, slots, valid, blocks, total):
    def step(i, x):
        parts = []
        for u in range(GROUP):
            at = (i * GROUP + u) * 2
            left = [jnp.where(valid[at + h] == 1, chosen[at + h], 0).astype(BF16) for h in range(2)]
            right = [window[slots[at + h]] for h in range(2)]
            parts.append(dot(jnp.concatenate(left, axis=1), jnp.concatenate(right, axis=0)))
        for u in range(GROUP):
            b = blocks[i * GROUP + u]
            total[b] = total[b] + parts[u]
        return x

    lax.fori_loop(0, steps, step, 0)


def near_kernel(sources, counts, *refs):
    buffers, (mats, out, *scratch) = refs[:-9], refs[-9:]
    window, chosen, slots, valid, blocks, sems, mat_sem = scratch
    steps = gather_near(0, sources, counts, buffers, mats, window, chosen, slots, valid, blocks, sems, mat_sem)
    out[...] = jnp.zeros_like(out)
    multiply_near(steps, window, chosen, slots, valid, blocks, out)


def last_kernel(first, sources, counts, *refs):
    buffers, (mats, near, evals, local, out, spread, turned, *scratch) = refs[:-14], refs[-14:]
    window, chosen, slots, valid, blocks, sems, mat_sem = scratch
    steps = gather_near(first, sources, counts, buffers, mats, window, chosen, slots, valid, blocks, sems, mat_sem)
    spread[...] = local[...].astype(F32)
    for j in range(2):
        turned[128 * j : 128 * j + 128, :] = spread[pl.ds(j, 256, stride=2), :].T.astype(BF16)
    for b in range(0, near.shape[0], 2):
        far = dot(evals[b : b + 2].reshape(256, 256), turned[...])
        out[b : b + 2] = near[b : b + 2] + far.reshape(2, 128, 256)
    multiply_near(steps, window, chosen, slots, valid, blocks, out)


def call_moment(charges, maps, lists, weights):
    vmem, hbm = pl.BlockSpec(memory_space=pltpu.VMEM), pl.BlockSpec(memory_space=pltpu.HBM)
    return pl.pallas_call(
        moment_kernel,
        out_shape=[jax.ShapeDtypeStruct((1024, 128), BF16)] + [pltpu.VMEM(w.shape, BF16) for w in weights],
        in_specs=[vmem] * (2 + len(lists)) + [hbm] * len(weights),
        out_specs=[vmem] * (1 + len(weights)),
        scratch_shapes=[pltpu.VMEM((8, 128), F32), pltpu.VMEM((1024, 128), F32), pltpu.SemaphoreType.DMA((3,))],
        compiler_params=pltpu.CompilerParams(vmem_limit_bytes=56 << 20),
        name="moment",
    )(charges, maps, *lists, *weights)


def call_far(received, weights):
    return pl.pallas_call(
        far_kernel,
        out_shape=jax.ShapeDtypeStruct((512, 128), BF16),
        in_specs=[pl.BlockSpec(memory_space=pltpu.VMEM)] * (1 + len(weights)),
        out_specs=pl.BlockSpec(memory_space=pltpu.VMEM),
        compiler_params=pltpu.CompilerParams(vmem_limit_bytes=24 << 20),
        name="far",
    )(received, *weights)


def near_scratch(buffers):
    return [
        pltpu.VMEM((12 * len(buffers), 128, 256), BF16),
        pltpu.VMEM((192 + 2 * GROUP, 128, 128), BF16),
        pltpu.SMEM((192 + 2 * GROUP,), jnp.int32),
        pltpu.SMEM((192 + 2 * GROUP,), jnp.int32),
        pltpu.SMEM((96 + GROUP,), jnp.int32),
        pltpu.SemaphoreType.DMA((len(buffers),)),
        pltpu.SemaphoreType.DMA,
    ]


def call_near(sources, counts, buffers, mats):
    smem, vmem, hbm = (pl.BlockSpec(memory_space=m) for m in (pltpu.SMEM, pltpu.VMEM, pltpu.HBM))
    return pl.pallas_call(
        near_kernel,
        out_shape=jax.ShapeDtypeStruct((mats.shape[0], 128, 256), F32),
        in_specs=[smem, smem] + [hbm] * (len(buffers) + 1),
        out_specs=vmem,
        scratch_shapes=near_scratch(buffers),
        compiler_params=pltpu.CompilerParams(vmem_limit_bytes=58 << 20),
        name="near",
    )(sources, counts, *buffers, mats)


def call_last(sources, counts, buffers, mats, near, evals, local):
    smem, vmem, hbm = (pl.BlockSpec(memory_space=m) for m in (pltpu.SMEM, pltpu.VMEM, pltpu.HBM))
    return pl.pallas_call(
        functools.partial(last_kernel, 144 - 12 * len(buffers)),
        out_shape=jax.ShapeDtypeStruct((mats.shape[0], 128, 256), F32),
        in_specs=[smem, smem] + [hbm] * (len(buffers) + 1) + [vmem] * 3,
        out_specs=vmem,
        scratch_shapes=[pltpu.VMEM((512, 128), F32), pltpu.VMEM((256, 256), BF16)] + near_scratch(buffers),
        compiler_params=pltpu.CompilerParams(vmem_limit_bytes=24 << 20),
        name="last",
    )(sources, counts, *buffers, mats, near, evals, local)


def flat(pairs):
    return [(a * 4 + b, c * 4 + d) for (a, b), (c, d) in pairs]


def outer(leaf):
    return leaf + 1 if leaf % 2 else leaf - 1


def outer_pairs(leaves, turn):
    return flat(
        [
            ((leaf, y), (outer(leaf), (y + turn) % 4))
            for leaf in range(leaves)
            for y in range(4)
            if 0 <= outer(leaf) < leaves
        ]
    )


def inner_pairs(leaves):
    return flat([((leaf, y), (leaf ^ 1, y)) for leaf in range(leaves) for y in range(4)])


def on_device(
    charges,
    near_mat,
    near_source,
    near_count,
    moment_map,
    local_eval,
    upward_child_translation,
    shift_down,
    transfer_ops,
    subtree_interaction_list,
    subtree_interaction_operators,
    parent_list,
    parent_ops,
):
    leaves = lax.axis_size("leaf")
    ring = [(i, (i + 1) % 4) for i in range(4)]
    back = [((i + 1) % 4, i) for i in range(4)]
    inner = inner_pairs(leaves)

    below = lax.ppermute(charges, "level", ring)
    above = lax.ppermute(charges, "level", back)
    outer_own = lax.ppermute(charges, BOTH, outer_pairs(leaves, 0))
    inner_own = lax.ppermute(charges, BOTH, inner)

    lists = (subtree_interaction_list, subtree_interaction_operators, parent_list, parent_ops)
    message, *weights = call_moment(charges, moment_map, lists, (upward_child_translation, transfer_ops, shift_down))
    received = lax.all_to_all(message.reshape(256, 4, 128), BOTH, 0, 0, tiled=True).reshape(1024, 128)

    outer_below = lax.ppermute(below, BOTH, outer_pairs(leaves, 0))
    outer_above = lax.ppermute(above, BOTH, outer_pairs(leaves, 0))
    far_own = lax.ppermute(below, "level", ring)
    outer_far = lax.ppermute(above, BOTH, outer_pairs(leaves, -1))
    inner_below = lax.ppermute(below, BOTH, inner)
    inner_above = lax.ppermute(above, BOTH, inner)

    columns = call_far(received, weights)
    inner_far = lax.ppermute(far_own, BOTH, inner)

    local = lax.all_to_all(columns.reshape(256, 2, 128), BOTH, 0, 0, tiled=True).reshape(512, 128)

    near_mat = pltpu.with_memory_space_constraint(near_mat, pltpu.HBM)
    early = [charges, above, far_own, below, inner_own, inner_above, inner_below, outer_own]
    late = [inner_far, outer_above, outer_far, outer_below]
    near = call_near(near_source, near_count, early, near_mat)
    return call_last(near_source, near_count, late, near_mat, near, local_eval, local)


def solution(mesh):
    placed = (
        P(("leaf", "level"), None, None),
        P(("leaf", "level"), None, None, None),
        P(("leaf", "level"), None),
        P(("leaf", "level")),
        P(("leaf", "level"), None, None),
        P(("leaf", "level"), None, None),
        P(),
        P(),
        P(),
        P("leaf", None),
        P("leaf", None),
        P("leaf", None),
        P("leaf", None),
    )
    return jax.shard_map(
        on_device,
        mesh=mesh,
        in_specs=placed,
        out_specs=P(("leaf", "level"), None, None),
        check_vma=False,
    )
```

time: 97.1 us -> 107 us (1.10)
  the two profiles are of different devices: /device:TPU:103 before, /device:TPU:1 now
where the time goes in v2:
time: 107 us
  starting transfers between devices  32.5 us (30%)
  blocking collectives  27.1 us (25%)
  waiting for transfers between devices  23.4 us (22%)
  Pallas kernels  21 us (20%)
  local copies, waits for them, and re-layouts  2.31 us (2%)
    all_to_all x1, blocking collectives, on_device(): lax.all_to_all(message.reshape(256, 4, 128), BOTH, 0, 0, tiled=True)  27.1 us
    ppermute x1, waiting for transfers between devices, on_device(): below = lax.ppermute(charges, 'level', ring)  11.3 us
    ppermute x1, starting transfers between devices, on_device(): outer_below = lax.ppermute(below, BOTH, outer_pairs(leaves, 0))  7.86 us
    pallas_call x1, Pallas kernels, call_near(): pl.pallas_call(near_kernel, out_shape=jax.ShapeDtypeStruct((mats.shape[0]...  7.56 us
    ppermute x1, waiting for transfers between devices, on_device(): far_own = lax.ppermute(below, 'level', ring)  6.86 us
    pallas_call x1, Pallas kernels, call_last(): pl.pallas_call(functools.partial(last_kernel, 144 - 12 * len(buffers)), o...  6.52 us
    all_to_all x1, starting transfers between devices, on_device(): lax.all_to_all(columns.reshape(256, 2, 128), BOTH, 0, 0, tiled=True)  5.44 us
    all_to_all x1, waiting for transfers between devices, on_device(): lax.all_to_all(columns.reshape(256, 2, 128), BOTH, 0, 0, tiled=True)  5.17 us
  transfers between devices with their start and end apart: 12, of which 3 were waited for; matrix products, arithmetic and copies ran while one was open for 0% of the time, Pallas kernels for 14%

profile of v2, /device:TPU:1, one launch (start us, length us, event | category | flops | bytes accessed | tf_op | source)
XLA Modules:
  0.0 106.6 jit_solution(10902573136593114890)
XLA Ops:
  0.0 2.1 %collective-permute-start = (bf16[12,128,256]{2,1,0:T(8,128)(2,1)}, bf16[12,128,256]{2,1,0:T(8,128)(2,1)}, u32[]{:S(2)}, u32[]{:S(2)}) collective-permute-start(bf16[12,128,256]{2,1,0:T(8,128)(2,1)} %charges.1), channel_id=1, source_target_pairs={{0,1},{1,2},{2,3},{3,0},{4,5},{5,6},{6,7},{7,4},{8,9},{9,10},{10,1... | collective-permute-start | bytes 2359304 | tf_op jit(solution)/shard_map/ppermute | solution.py:324
  2.1 1.4 %collective-permute-start.3 = (bf16[12,128,256]{2,1,0:T(8,128)(2,1)}, bf16[12,128,256]{2,1,0:T(8,128)(2,1)}, u32[]{:S(2)}, u32[]{:S(2)}) collective-permute-start(bf16[12,128,256]{2,1,0:T(8,128)(2,1)} %charges.1), channel_id=1, source_target_pairs={{1,0},{2,1},{3,2},{0,3},{5,4},{6,5},{7,6},{4,7},{9,8},{10,9},{11,1... | collective-permute-start | bytes 2359304 | tf_op jit(solution)/shard_map/ppermute | solution.py:325
  3.6 4.2 %collective-permute-start.10 = (bf16[12,128,256]{2,1,0:T(8,128)(2,1)}, bf16[12,128,256]{2,1,0:T(8,128)(2,1)S(1)}, u32[]{:S(2)}, u32[]{:S(2)}) collective-permute-start(bf16[12,128,256]{2,1,0:T(8,128)(2,1)} %charges.1), channel_id=1, source_target_pairs={{4,8},{5,9},{6,10},{7,11},{8,4},{9,5},{10,6},{11,7},{12,16},{13,17... | collective-permute-start | bytes 2359304 | tf_op jit(solution)/shard_map/ppermute | solution.py:326
  7.7 0.1 collective-permute-start.7
  7.8 11.3 %collective-permute-done.refs_3_ = bf16[12,128,256]{2,1,0:T(8,128)(2,1)} collective-permute-done((bf16[12,128,256]{2,1,0:T(8,128)(2,1)}, bf16[12,128,256]{2,1,0:T(8,128)(2,1)}, u32[]{:S(2)}, u32[]{:S(2)}) %collective-permute-start) | collective-permute-done | bytes 786464 | tf_op jit(solution)/shard_map/ppermute | solution.py:324
  19.2 1.5 %collective-permute-start.1 = (bf16[12,128,256]{2,1,0:T(8,128)(2,1)}, bf16[12,128,256]{2,1,0:T(8,128)(2,1)}, u32[]{:S(2)}, u32[]{:S(2)}) collective-permute-start(bf16[12,128,256]{2,1,0:T(8,128)(2,1)} %collective-permute-done.refs_3_), channel_id=1, source_target_pairs={{0,1},{1,2},{2,3},{3,0},{4,5},{5,6},{6,7},{7,4},{8,9},{9,10},{10,1... | collective-permute-start | bytes 2359304 | tf_op jit(solution)/shard_map/ppermute | solution.py:335
  20.7 1.9 %collective-permute-start.8 = (bf16[12,128,256]{2,1,0:T(8,128)(2,1)}, bf16[12,128,256]{2,1,0:T(8,128)(2,1)S(1)}, u32[]{:S(2)}, u32[]{:S(2)}) collective-permute-start(bf16[12,128,256]{2,1,0:T(8,128)(2,1)} %collective-permute-done.3.refs_1_), channel_id=1, source_target_pairs={{0,4},{1,5},{2,6},{3,7},{4,0},{5,1},{6,2},{7,3},{8,12},{9,13},{10,... | collective-permute-start | bytes 2359304 | tf_op jit(solution)/shard_map/ppermute | solution.py:338
  22.7 3.5 %collective-permute-start.4 = (bf16[12,128,256]{2,1,0:T(8,128)(2,1)}, bf16[12,128,256]{2,1,0:T(8,128)(2,1)S(1)}, u32[]{:S(2)}, u32[]{:S(2)}) collective-permute-start(bf16[12,128,256]{2,1,0:T(8,128)(2,1)} %collective-permute-done.3.refs_1_), channel_id=1, source_target_pairs={{4,8},{5,9},{6,10},{7,11},{8,4},{9,5},{10,6},{11,7},{12,16},{13,17... | collective-permute-start | bytes 2359304 | tf_op jit(solution)/shard_map/ppermute | solution.py:334
  26.2 4.4 %collective-permute-start.5 = (bf16[12,128,256]{2,1,0:T(8,128)(2,1)}, bf16[12,128,256]{2,1,0:T(8,128)(2,1)S(1)}, u32[]{:S(2)}, u32[]{:S(2)}) collective-permute-start(bf16[12,128,256]{2,1,0:T(8,128)(2,1)} %collective-permute-done.3.refs_1_), channel_id=1, source_target_pairs={{4,11},{5,8},{6,9},{7,10},{8,7},{9,4},{10,5},{11,6},{12,19},{13,16... | collective-permute-start | bytes 2359304 | tf_op jit(solution)/shard_map/ppermute | solution.py:336
  30.6 6.9 %collective-permute-done.1.refs_2_ = bf16[12,128,256]{2,1,0:T(8,128)(2,1)} collective-permute-done((bf16[12,128,256]{2,1,0:T(8,128)(2,1)}, bf16[12,128,256]{2,1,0:T(8,128)(2,1)}, u32[]{:S(2)}, u32[]{:S(2)}) %collective-permute-start.1) | collective-permute-done | bytes 786464 | tf_op jit(solution)/shard_map/ppermute | solution.py:335
  37.5 7.9 %collective-permute-start.6 = (bf16[12,128,256]{2,1,0:T(8,128)(2,1)}, bf16[12,128,256]{2,1,0:T(8,128)(2,1)S(1)}, u32[]{:S(2)}, u32[]{:S(2)}) collective-permute-start(bf16[12,128,256]{2,1,0:T(8,128)(2,1)} %collective-permute-done.refs_3_), channel_id=1, source_target_pairs={{4,8},{5,9},{6,10},{7,11},{8,4},{9,5},{10,6},{11,7},{12,16},{13,17... | collective-permute-start | bytes 2359304 | tf_op jit(solution)/shard_map/ppermute | solution.py:333
  45.4 0.9 copy-done.6
  46.3 4.0 %moment.1 = (bf16[1024,128]{1,0:T(8,128)(2,1)}, bf16[8,256,256]{2,1,0:T(8,128)(2,1)S(1)}, bf16[8,256,256]{2,1,0:T(8,128)(2,1)S(1)}, bf16[8,256,256]{2,1,0:T(8,128)(2,1)S(1)}) custom-call(bf16[12,128,256]{2,1,0:T(8,128)(2,1)} %charges.1, bf16[12,256,128]{2,1,0:T(8,128)(2,1)} %maps.1, s32[1,32]{1,0:T(1,128)} %cells.1, s32[1,32]{1,0:T(1,128)} %ops.1, ...), custom_call_target="tpu_custom_call" | custom-call | tf_op jit(solution)/shard_map/moment/pallas_call | solution.py:221
  50.3 27.1 %all_to_all.10 = bf16[256,4,128]{2,1,0:T(4,128)(2,1)S(1)} all-to-all(bf16[256,4,128]{2,1,0:T(4,128)(2,1)} %bitcast.6), channel_id=1, replica_groups=mesh['leaf'=64,'level'=4] {'leaf','level'}, dimensions={0} | all-to-all | bytes 524288 | tf_op jit(solution)/shard_map/all_to_all | solution.py:331
  77.4 2.9 %far.1 = bf16[512,128]{1,0:T(8,128)(2,1)} custom-call(bf16[1024,128]{1,0:T(8,128)(2,1)S(1)} %bitcast.4, bf16[8,256,256]{2,1,0:T(8,128)(2,1)S(1)} %get-tuple-element.10.upward, bf16[8,256,256]{2,1,0:T(8,128)(2,1)S(1)} %get-tuple-element.11.transfer, bf16[8,256,256]{2,1,0:T(8,128)(2,1)S(1)} %get-tuple-element.12.shift), custom_call_target="tpu_custom_call" | custom-call | tf_op jit(solution)/shard_map/far/pallas_call | solution.py:233
  80.4 5.4 %all-to-all-start.1 = ((bf16[256,2,128]{2,1,0:T(2,128)(2,1)}), bf16[256,2,128]{2,1,0:T(2,128)(2,1)S(1)}, u32[]{:S(2)}, u32[]{:S(2)}) async-start(bf16[256,2,128]{2,1,0:T(2,128)(2,1)} %bitcast.2), calls=%async_computation.1 | async-start | bytes 262144 | tf_op jit(solution)/shard_map/all_to_all | solution.py:343
  85.8 0.0 copy-start.1
  85.8 0.0 copy-start.2
  85.8 0.0 copy-start.3
  85.9 7.6 %near.1.refs_5_ = f32[12,128,256]{2,1,0:T(8,128)} custom-call(s32[12,16]{1,0:T(8,128)} %sources.3, s32[12]{0:T(128)} %counts.3, bf16[12,128,256]{2,1,0:T(8,128)(2,1)} %charges.1, bf16[12,128,256]{2,1,0:T(8,128)(2,1)} %collective-permute-done.3.refs_1_, bf16[12,128,256]{2,1,0:T(8,128)(2,1)} %collective-permute-done.1.refs_2_, ...), custom_call_target="tpu_custom_call" | custom-call | tf_op jit(solution)/shard_map/near/pallas_call | solution.py:257
  93.4 5.2 %all-to-all-done.1 = bf16[256,2,128]{2,1,0:T(2,128)(2,1)S(1)} async-done(((bf16[256,2,128]{2,1,0:T(2,128)(2,1)}), bf16[256,2,128]{2,1,0:T(2,128)(2,1)S(1)}, u32[]{:S(2)}, u32[]{:S(2)}) %all-to-all-start.1) | async-done | bytes 131104 | tf_op jit(solution)/shard_map/all_to_all | solution.py:343
  98.6 0.0 copy-start
  98.7 1.4 %copy-done = f32[12,128,256]{2,1,0:T(8,128)S(1)} copy-done((f32[12,128,256]{2,1,0:T(8,128)S(1)}, f32[12,128,256]{2,1,0:T(8,128)}, u32[]{:S(2)}) %copy-start) | copy-done | bytes 1572888
  100.1 6.5 %last.1 = f32[12,128,256]{2,1,0:T(8,128)} custom-call(s32[12,16]{1,0:T(8,128)S(1)} %copy-done.2, s32[12]{0:T(128)S(1)} %copy-done.3, bf16[12,128,256]{2,1,0:T(8,128)(2,1)} %collective-permute-done.2.refs_0_, bf16[12,128,256]{2,1,0:T(8,128)(2,1)S(1)} %collective-permute-done.4.refs_1_, bf16[12,128,256]{2,1,0:T(8,128)(2,1)S(1)} %collective-permute-done.5.refs_2_, ...), custom_call_target="tpu_custom_call" | custom-call | tf_op jit(solution)/shard_map/last/pallas_call | solution.py:270
  (19 shorter events, 0.0 us)
Async XLA Ops:
  0.0 19.2 %collective-permute-start = (bf16[12,128,256]{2,1,0:T(8,128)(2,1)}, bf16[12,128,256]{2,1,0:T(8,128)(2,1)}, u32[]{:S(2)}, u32[]{:S(2)}) collective-permute-start(bf16[12,128,256]{2,1,0:T(8,128)(2,1)} %charges.1), channel_id=1, source_target_pairs={{0,1},{1,2},{2,3},{3,0},{4,5},{5,6},{6,7},{7,4},{8,9},{9,10},{10,1... | collective-permute-start | bytes 2359304 | tf_op jit(solution)/shard_map/ppermute | solution.py:324
  2.1 18.6 %collective-permute-start.3 = (bf16[12,128,256]{2,1,0:T(8,128)(2,1)}, bf16[12,128,256]{2,1,0:T(8,128)(2,1)}, u32[]{:S(2)}, u32[]{:S(2)}) collective-permute-start(bf16[12,128,256]{2,1,0:T(8,128)(2,1)} %charges.1), channel_id=1, source_target_pairs={{1,0},{2,1},{3,2},{0,3},{5,4},{6,5},{7,6},{4,7},{9,8},{10,9},{11,1... | collective-permute-start | bytes 2359304 | tf_op jit(solution)/shard_map/ppermute | solution.py:325
  3.6 19.1 %collective-permute-start.10 = (bf16[12,128,256]{2,1,0:T(8,128)(2,1)}, bf16[12,128,256]{2,1,0:T(8,128)(2,1)S(1)}, u32[]{:S(2)}, u32[]{:S(2)}) collective-permute-start(bf16[12,128,256]{2,1,0:T(8,128)(2,1)} %charges.1), channel_id=1, source_target_pairs={{4,8},{5,9},{6,10},{7,11},{8,4},{9,5},{10,6},{11,7},{12,16},{13,17... | collective-permute-start | bytes 2359304 | tf_op jit(solution)/shard_map/ppermute | solution.py:326
  7.7 18.5 %collective-permute-start.7 = (bf16[12,128,256]{2,1,0:T(8,128)(2,1)}, bf16[12,128,256]{2,1,0:T(8,128)(2,1)S(1)}, u32[]{:S(2)}, u32[]{:S(2)}) collective-permute-start(bf16[12,128,256]{2,1,0:T(8,128)(2,1)} %charges.1), channel_id=1, source_target_pairs={{0,4},{1,5},{2,6},{3,7},{4,0},{5,1},{6,2},{7,3},{8,12},{9,13},{10,... | collective-permute-start | bytes 2359304 | tf_op jit(solution)/shard_map/ppermute | solution.py:327
  19.2 18.3 %collective-permute-start.1 = (bf16[12,128,256]{2,1,0:T(8,128)(2,1)}, bf16[12,128,256]{2,1,0:T(8,128)(2,1)}, u32[]{:S(2)}, u32[]{:S(2)}) collective-permute-start(bf16[12,128,256]{2,1,0:T(8,128)(2,1)} %collective-permute-done.refs_3_), channel_id=1, source_target_pairs={{0,1},{1,2},{2,3},{3,0},{4,5},{5,6},{6,7},{7,4},{8,9},{9,10},{10,1... | collective-permute-start | bytes 2359304 | tf_op jit(solution)/shard_map/ppermute | solution.py:335
  20.7 24.7 %collective-permute-start.8 = (bf16[12,128,256]{2,1,0:T(8,128)(2,1)}, bf16[12,128,256]{2,1,0:T(8,128)(2,1)S(1)}, u32[]{:S(2)}, u32[]{:S(2)}) collective-permute-start(bf16[12,128,256]{2,1,0:T(8,128)(2,1)} %collective-permute-done.3.refs_1_), channel_id=1, source_target_pairs={{0,4},{1,5},{2,6},{3,7},{4,0},{5,1},{6,2},{7,3},{8,12},{9,13},{10,... | collective-permute-start | bytes 2359304 | tf_op jit(solution)/shard_map/ppermute | solution.py:338
  22.7 63.2 %collective-permute-start.9 = (bf16[12,128,256]{2,1,0:T(8,128)(2,1)}, bf16[12,128,256]{2,1,0:T(8,128)(2,1)}, u32[]{:S(2)}, u32[]{:S(2)}) collective-permute-start(bf16[12,128,256]{2,1,0:T(8,128)(2,1)} %collective-permute-done.refs_3_), channel_id=1, source_target_pairs={{0,4},{1,5},{2,6},{3,7},{4,0},{5,1},{6,2},{7,3},{8,12},{9,13},{10,... | collective-permute-start | bytes 2359304 | tf_op jit(solution)/shard_map/ppermute | solution.py:337
  22.7 22.7 %copy-start.4 = (bf16[12,128,256]{2,1,0:T(8,128)(2,1)}, bf16[12,128,256]{2,1,0:T(8,128)(2,1)S(1)}, u32[]{:S(2)}) copy-start(bf16[12,128,256]{2,1,0:T(8,128)(2,1)S(1)} %collective-permute-done.10.refs_7_) | copy-start | bytes 2359300
  22.7 75.9 %collective-permute-start.4 = (bf16[12,128,256]{2,1,0:T(8,128)(2,1)}, bf16[12,128,256]{2,1,0:T(8,128)(2,1)S(1)}, u32[]{:S(2)}, u32[]{:S(2)}) collective-permute-start(bf16[12,128,256]{2,1,0:T(8,128)(2,1)} %collective-permute-done.3.refs_1_), channel_id=1, source_target_pairs={{4,8},{5,9},{6,10},{7,11},{8,4},{9,5},{10,6},{11,7},{12,16},{13,17... | collective-permute-start | bytes 2359304 | tf_op jit(solution)/shard_map/ppermute | solution.py:334
  26.2 19.2 %copy-start.5 = (bf16[12,128,256]{2,1,0:T(8,128)(2,1)}, bf16[12,128,256]{2,1,0:T(8,128)(2,1)S(1)}, u32[]{:S(2)}) copy-start(bf16[12,128,256]{2,1,0:T(8,128)(2,1)S(1)} %collective-permute-done.7.refs_4_) | copy-start | bytes 2359300
  26.2 72.4 %collective-permute-start.5 = (bf16[12,128,256]{2,1,0:T(8,128)(2,1)}, bf16[12,128,256]{2,1,0:T(8,128)(2,1)S(1)}, u32[]{:S(2)}, u32[]{:S(2)}) collective-permute-start(bf16[12,128,256]{2,1,0:T(8,128)(2,1)} %collective-permute-done.3.refs_1_), channel_id=1, source_target_pairs={{4,11},{5,8},{6,9},{7,10},{8,7},{9,4},{10,5},{11,6},{12,19},{13,16... | collective-permute-start | bytes 2359304 | tf_op jit(solution)/shard_map/ppermute | solution.py:336
  37.5 61.1 %collective-permute-start.6 = (bf16[12,128,256]{2,1,0:T(8,128)(2,1)}, bf16[12,128,256]{2,1,0:T(8,128)(2,1)S(1)}, u32[]{:S(2)}, u32[]{:S(2)}) collective-permute-start(bf16[12,128,256]{2,1,0:T(8,128)(2,1)} %collective-permute-done.refs_3_), channel_id=1, source_target_pairs={{4,8},{5,9},{6,10},{7,11},{8,4},{9,5},{10,6},{11,7},{12,16},{13,17... | collective-permute-start | bytes 2359304 | tf_op jit(solution)/shard_map/ppermute | solution.py:333
  45.4 0.9 copy-start.6
  46.3 52.3 %collective-permute-start.2 = (bf16[12,128,256]{2,1,0:T(8,128)(2,1)}, bf16[12,128,256]{2,1,0:T(8,128)(2,1)}, u32[]{:S(2)}, u32[]{:S(2)}) collective-permute-start(bf16[12,128,256]{2,1,0:T(8,128)(2,1)} %collective-permute-done.1.refs_2_), channel_id=1, source_target_pairs={{0,4},{1,5},{2,6},{3,7},{4,0},{5,1},{6,2},{7,3},{8,12},{9,13},{10,... | collective-permute-start | bytes 2359304 | tf_op jit(solution)/shard_map/ppermute | solution.py:341
  80.4 18.2 %all-to-all-start.1 = ((bf16[256,2,128]{2,1,0:T(2,128)(2,1)}), bf16[256,2,128]{2,1,0:T(2,128)(2,1)S(1)}, u32[]{:S(2)}, u32[]{:S(2)}) async-start(bf16[256,2,128]{2,1,0:T(2,128)(2,1)} %bitcast.2), calls=%async_computation.1 | async-start | bytes 262144 | tf_op jit(solution)/shard_map/all_to_all | solution.py:343
  85.8 12.8 %copy-start.1 = (bf16[12,128,256]{2,1,0:T(8,128)(2,1)S(1)}, bf16[12,128,256]{2,1,0:T(8,128)(2,1)}, u32[]{:S(2)}) copy-start(bf16[12,128,256]{2,1,0:T(8,128)(2,1)} %refs_6_.1) | copy-start | bytes 2359300
  85.8 12.8 %copy-start.2 = (s32[12,16]{1,0:T(8,128)S(1)}, s32[12,16]{1,0:T(8,128)}, u32[]{:S(2)}) copy-start(s32[12,16]{1,0:T(8,128)} %sources.3) | copy-start | bytes 2308
  85.8 12.8 %copy-start.3 = (s32[12]{0:T(128)S(1)}, s32[12]{0:T(128)}, u32[]{:S(2)}) copy-start(s32[12]{0:T(128)} %counts.3) | copy-start | bytes 148
  98.6 1.4 %copy-start = (f32[12,128,256]{2,1,0:T(8,128)S(1)}, f32[12,128,256]{2,1,0:T(8,128)}, u32[]{:S(2)}) copy-start(f32[12,128,256]{2,1,0:T(8,128)} %near.1.refs_5_) | copy-start | bytes 4718596

commit v3 on v2

v3 whole, which is shorter than its diff:
```python
import functools

import jax
import jax.numpy as jnp
from jax import lax
from jax.experimental import pallas as pl
from jax.experimental.pallas import tpu as pltpu
from jax.sharding import PartitionSpec as P


BOTH = ("leaf", "level")
NT = (((1,), (1,)), ((), ()))
F32 = jnp.float32
BF16 = jnp.bfloat16
GROUP = 4


def dot(a, b):
    return jnp.dot(a, b, preferred_element_type=F32)


def dot_nt(a, b):
    return lax.dot_general(a, b, NT, preferred_element_type=F32)


def moment_kernel(charges, maps, cells, ops, parents, parent_ops, out, row, spread):
    blocks = charges.shape[0]
    total = None
    for b in range(0, blocks, 2):
        left = jnp.concatenate([maps[b], maps[b + 1]], axis=1)
        right = jnp.concatenate([charges[b], charges[b + 1]], axis=0)
        part = dot(left, right)
        total = part if total is None else total + part
    turned = total.T
    row[...] = jnp.zeros_like(row)
    row[0:1, 0:32] = ((cells[...] & 7) * 8 + (cells[...] >> 3)).astype(F32)
    row[0:1, 32:64] = ops[...].astype(F32)
    row[0:1, 64:72] = parents[...].astype(F32)
    row[0:1, 72:80] = parent_ops[...].astype(F32)
    for j in range(2):
        spread[pl.ds(j, 256, stride=4), :] = turned[:, 128 * j : 128 * j + 128]
    spread[pl.ds(2, 256, stride=4), :] = jnp.broadcast_to(row[0:1, :], (256, 128))
    spread[pl.ds(3, 256, stride=4), :] = jnp.zeros((256, 128), F32)
    out[...] = spread[...].astype(BF16)


def iota(shape, dim):
    return lax.broadcasted_iota(jnp.int32, shape, dim)


def split(x):
    high = x.astype(BF16)
    return high, (x - high.astype(F32)).astype(BF16)


def far_kernel(received, upward, transfer, shift_hbm, out, shift, sem):
    copy = pltpu.make_async_copy(shift_hbm, shift, sem)
    copy.start()
    rows, cols = iota((64, 1024), 0), iota((64, 1024), 1)
    cell = (rows & 7) * 8 + (rows >> 3)
    chosen = []
    for j in range(2):
        chosen.append(jnp.where(((cols >> 4) == cell) & ((cols & 3) == j), 1.0, 0.0))
    chosen.append(jnp.where(cols == cell * 16 + 2, 1.0, 0.0))
    gathered = dot(jnp.concatenate(chosen, axis=0).astype(BF16), received[...])
    moments = jnp.concatenate([gathered[0:64], gathered[64:128]], axis=1).astype(BF16)
    lists = gathered[128:192]
    lane = iota((64, 128), 1).astype(F32)

    codes = lists[:, 32:64] * 64.0 + lists[:, 0:32]
    counts = [jnp.zeros((64, 128), F32) for _ in range(4)]
    for k in range(32):
        code = jnp.broadcast_to(codes[:, k : k + 1], (64, 128)) - lane
        for g in range(4):
            counts[g] = counts[g] + jnp.where(code == 128.0 * g, 1.0, 0.0)
    parent_codes = lists[:, 72:80] * 8.0 + lists[:, 64:72]
    parent_counts = jnp.zeros((64, 128), F32)
    for k in range(8):
        code = jnp.broadcast_to(parent_codes[:, k : k + 1], (64, 128))
        parent_counts = parent_counts + jnp.where(code == lane, 1.0, 0.0)

    first = lane < 64.0
    picks = []
    for g in range(4):
        picks.append(jnp.where(first, counts[g], 0.0))
        picks.append(jnp.where(first, 0.0, counts[g]))
    picks = jnp.concatenate(picks, axis=0).astype(BF16)
    sums = dot(picks, jnp.concatenate([moments, moments], axis=0))
    high, low = split(sums)

    copy.wait()
    wide = moments.astype(F32)
    upper = jnp.zeros((8, 256), F32)
    for i in range(8):
        upper = upper + dot_nt(wide[8 * i : 8 * i + 8].astype(BF16), upward[i])
    upper = upper.astype(BF16)

    far = jnp.zeros((64, 256), F32)
    moved = []
    for o in range(8):
        both = jnp.concatenate([high[64 * o : 64 * o + 64], low[64 * o : 64 * o + 64]], axis=0)
        part = dot_nt(both, transfer[o])
        far = far + part[0:64] + part[64:128]
        moved.append(dot_nt(upper, transfer[o]))
    moved_high, moved_low = split(jnp.concatenate(moved, axis=0))
    weights = parent_counts[:, 0:64].astype(BF16)
    coarse = dot(weights, moved_high) + dot(weights, moved_low)
    coarse = coarse.astype(BF16).astype(F32)
    down = [dot_nt(coarse[8 * j : 8 * j + 8].astype(BF16), shift[j]) for j in range(8)]
    local = (far + jnp.concatenate(down, axis=0)).astype(BF16)

    rows, cols = iota((512, 128), 0), iota((512, 128), 1)
    cell = (cols & 7) * 8 + ((cols >> 3) & 7)
    spread = jnp.where(((rows >> 3) == cell) & ((rows & 1) == (cols >> 6)), 1.0, 0.0).astype(BF16)
    out[...] = dot(spread, jnp.concatenate([local[:, 0:128], local[:, 128:256]], axis=0)).astype(BF16)


def list_near(early, sources, counts, mats, lists, chosen, sem):
    level, odd_leaf = lax.axis_index("level"), lax.axis_index("leaf") & 1

    def place(source):
        subtree = jnp.where(source >= 48, 1, 0) + jnp.where(source >= 96, 1, 0)
        block = source - 48 * subtree
        quarter = (block * 43) >> 9
        is_inner = (subtree == 0) == (odd_leaf == 1)
        group = jnp.where(subtree == 1, 0, jnp.where(is_inner, 1, 2))
        at = group * 4 + ((quarter - level) & 3)
        at = jnp.where(at == 6, 8, jnp.where((at == 7) | (at == 8), at - 1, at))
        return at * 12 + block - 12 * quarter

    def add(which, source, b, k, n):
        if which == 0:
            pltpu.make_async_copy(mats.at[b, k], chosen.at[n], sem).start()
        lists[which][0, n] = source
        lists[which][1, n] = k + 1
        lists[which][2, n >> 1] = b

    def take(b, k, state):
        n0, n1 = state
        source = place(sources[b, k])
        is_late = source >= early

        @pl.when(is_late)
        def _():
            add(1, source - early, b, k, n1)

        @pl.when(jnp.logical_not(is_late))
        def _():
            add(0, source, b, k, n0)

        step = jnp.where(is_late, 1, 0)
        return n0 + 1 - step, n1 + step

    def take_block(b, state):
        starts, used = state[0:2], state[2:4]
        ends = lax.fori_loop(0, counts[b], functools.partial(take, b), starts)
        odd = [(end - start) & 1 for end, start in zip(ends, starts)]
        for which in range(2):

            @pl.when(odd[which] == 1)
            def _():
                lists[which][0, ends[which]] = 0
                lists[which][1, ends[which]] = 0

        used = tuple(u + end - start for u, end, start in zip(used, ends, starts))
        return tuple(end + o for end, o in zip(ends, odd)) + used

    state = lax.fori_loop(0, counts.shape[0], take_block, (jnp.int32(0),) * 4)
    for which in range(2):
        n = state[which]
        for extra in range(2 * GROUP):
            lists[which][0, n + extra] = 0
            lists[which][1, n + extra] = 0
            lists[which][2, (n + extra) >> 1] = 0
        lists[which][2, 255] = (n + 2 * GROUP - 1) // (2 * GROUP)
    return state[2]


def wait_chosen(used, mats, chosen, sem):
    def wait(_, x):
        pltpu.make_async_copy(mats.at[0, 0], chosen.at[0], sem).wait()
        return x

    lax.fori_loop(0, used, wait, 0)


def multiply_near(window, chosen, listed, total):
    def step(i, x):
        parts = []
        for u in range(GROUP):
            at = (i * GROUP + u) * 2
            left = [jnp.where(listed[1, at + h] > 0, chosen[at + h], 0).astype(BF16) for h in range(2)]
            right = [window[listed[0, at + h]] for h in range(2)]
            parts.append(dot(jnp.concatenate(left, axis=1), jnp.concatenate(right, axis=0)))
        for u in range(GROUP):
            b = listed[2, i * GROUP + u]
            total[b] = total[b] + parts[u]
        return x

    lax.fori_loop(0, listed[2, 255], step, 0)


def window_copies(buffers, window, sems):
    return [pltpu.make_async_copy(x, window.at[pl.ds(n * 12, 12)], sems.at[n]) for n, x in enumerate(buffers)]


def near_kernel(sources, counts, *refs):
    buffers, (mats, out, late, window, chosen, listed, sems, mat_sem) = refs[:-8], refs[-8:]
    copies = window_copies(buffers, window, sems)
    for copy in copies:
        copy.start()
    used = list_near(12 * len(buffers), sources, counts, mats, (listed, late), chosen, mat_sem)
    out[...] = jnp.zeros_like(out)
    wait_chosen(used, mats, chosen, mat_sem)
    for copy in copies:
        copy.wait()
    multiply_near(window, chosen, listed, out)


def last_kernel(late, *refs):
    buffers, (mats, near, evals, local, out, spread, turned, window, chosen, sems, mat_sem) = refs[:-11], refs[-11:]
    copies = window_copies(buffers, window, sems)
    for copy in copies:
        copy.start()

    def take(n, used):
        k = late[1, n]

        @pl.when(k > 0)
        def _():
            pltpu.make_async_copy(mats.at[late[2, n >> 1], k - 1], chosen.at[n], mat_sem).start()

        return used + jnp.where(k > 0, 1, 0)

    used = lax.fori_loop(0, late[2, 255] * 2 * GROUP, take, jnp.int32(0))
    spread[...] = local[...].astype(F32)
    for j in range(2):
        turned[128 * j : 128 * j + 128, :] = spread[pl.ds(j, 256, stride=2), :].T.astype(BF16)
    for b in range(0, near.shape[0], 2):
        far = dot(evals[b : b + 2].reshape(256, 256), turned[...])
        out[b : b + 2] = near[b : b + 2] + far.reshape(2, 128, 256)
    wait_chosen(used, mats, chosen, mat_sem)
    for copy in copies:
        copy.wait()
    multiply_near(window, chosen, late, out)


def call_moment(charges, maps, lists):
    vmem = pl.BlockSpec(memory_space=pltpu.VMEM)
    return pl.pallas_call(
        moment_kernel,
        out_shape=jax.ShapeDtypeStruct((1024, 128), BF16),
        in_specs=[vmem] * (2 + len(lists)),
        out_specs=vmem,
        scratch_shapes=[pltpu.VMEM((8, 128), F32), pltpu.VMEM((1024, 128), F32)],
        compiler_params=pltpu.CompilerParams(vmem_limit_bytes=58 << 20),
        name="moment",
    )(charges, maps, *lists)


def call_far(received, weights):
    return pl.pallas_call(
        far_kernel,
        out_shape=jax.ShapeDtypeStruct((512, 128), BF16),
        in_specs=[VMEM] * 3 + [HBM],
        out_specs=VMEM,
        scratch_shapes=[pltpu.VMEM(weights[2].shape, BF16), pltpu.SemaphoreType.DMA],
        compiler_params=pltpu.CompilerParams(vmem_limit_bytes=24 << 20),
        name="far",
    )(received, *weights)


SLOTS = 192 + 2 * GROUP
SMEM, VMEM, HBM = (pl.BlockSpec(memory_space=m) for m in (pltpu.SMEM, pltpu.VMEM, pltpu.HBM))


def call_near(sources, counts, buffers, mats):
    return pl.pallas_call(
        near_kernel,
        out_shape=[pltpu.VMEM((mats.shape[0], 128, 256), F32), jax.ShapeDtypeStruct((3, 256), jnp.int32)],
        in_specs=[SMEM, SMEM] + [HBM] * (len(buffers) + 1),
        out_specs=[VMEM, SMEM],
        scratch_shapes=[
            pltpu.VMEM((12 * len(buffers), 128, 256), BF16),
            pltpu.VMEM((SLOTS, 128, 128), BF16),
            pltpu.SMEM((3, 256), jnp.int32),
            pltpu.SemaphoreType.DMA((len(buffers),)),
            pltpu.SemaphoreType.DMA,
        ],
        compiler_params=pltpu.CompilerParams(vmem_limit_bytes=58 << 20),
        name="near",
    )(sources, counts, *buffers, mats)


def call_last(late, buffers, mats, near, evals, local):
    return pl.pallas_call(
        last_kernel,
        out_shape=jax.ShapeDtypeStruct(near.shape, F32),
        in_specs=[SMEM] + [HBM] * (len(buffers) + 1) + [VMEM] * 3,
        out_specs=VMEM,
        scratch_shapes=[
            pltpu.VMEM((512, 128), F32),
            pltpu.VMEM((256, 256), BF16),
            pltpu.VMEM((12 * len(buffers), 128, 256), BF16),
            pltpu.VMEM((SLOTS, 128, 128), BF16),
            pltpu.SemaphoreType.DMA((len(buffers),)),
            pltpu.SemaphoreType.DMA,
        ],
        compiler_params=pltpu.CompilerParams(vmem_limit_bytes=24 << 20),
        name="last",
    )(late, *buffers, mats, near, evals, local)


def permute(x, axes, pairs):
    return pltpu.with_memory_space_constraint(lax.ppermute(x, axes, pairs), pltpu.HBM)


def flat(pairs):
    return [(a * 4 + b, c * 4 + d) for (a, b), (c, d) in pairs]


def outer(leaf):
    return leaf + 1 if leaf % 2 else leaf - 1


def outer_pairs(leaves, turn):
    return flat(
        [
            ((leaf, y), (outer(leaf), (y + turn) % 4))
            for leaf in range(leaves)
            for y in range(4)
            if 0 <= outer(leaf) < leaves
        ]
    )


def inner_pairs(leaves):
    return flat([((leaf, y), (leaf ^ 1, y)) for leaf in range(leaves) for y in range(4)])


def on_device(
    charges,
    near_mat,
    near_source,
    near_count,
    moment_map,
    local_eval,
    upward_child_translation,
    shift_down,
    transfer_ops,
    subtree_interaction_list,
    subtree_interaction_operators,
    parent_list,
    parent_ops,
):
    leaves = lax.axis_size("leaf")
    ring = [(i, (i + 1) % 4) for i in range(4)]
    back = [((i + 1) % 4, i) for i in range(4)]
    inner = inner_pairs(leaves)

    below = permute(charges, "level", ring)
    above = permute(charges, "level", back)
    outer_own = permute(charges, BOTH, outer_pairs(leaves, 0))
    inner_own = permute(charges, BOTH, inner)

    lists = (subtree_interaction_list, subtree_interaction_operators, parent_list, parent_ops)
    message = call_moment(charges, moment_map, lists)
    shift_down = pltpu.with_memory_space_constraint(shift_down, pltpu.HBM)
    weights = (upward_child_translation, transfer_ops, shift_down)
    received = lax.all_to_all(message.reshape(256, 4, 128), BOTH, 0, 0, tiled=True).reshape(1024, 128)

    outer_below = permute(below, BOTH, outer_pairs(leaves, 0))
    outer_above = permute(above, BOTH, outer_pairs(leaves, 0))
    far_own = permute(below, "level", ring)
    outer_far = permute(above, BOTH, outer_pairs(leaves, -1))
    inner_below = permute(below, BOTH, inner)
    inner_above = permute(above, BOTH, inner)

    columns = call_far(received, weights)
    inner_far = permute(far_own, BOTH, inner)

    local = lax.all_to_all(columns.reshape(256, 2, 128), BOTH, 0, 0, tiled=True).reshape(512, 128)

    near_mat = pltpu.with_memory_space_constraint(near_mat, pltpu.HBM)
    early = [charges, above, far_own, below, inner_own, inner_above, inner_below, outer_own]
    late = [inner_far, outer_above, outer_far, outer_below]
    near, listed = call_near(near_source, near_count, early, near_mat)
    listed = pltpu.with_memory_space_constraint(listed, pltpu.HBM)
    return call_last(listed, late, near_mat, near, local_eval, local)


def solution(mesh):
    placed = (
        P(("leaf", "level"), None, None),
        P(("leaf", "level"), None, None, None),
        P(("leaf", "level"), None),
        P(("leaf", "level")),
        P(("leaf", "level"), None, None),
        P(("leaf", "level"), None, None),
        P(),
        P(),
        P(),
        P("leaf", None),
        P("leaf", None),
        P("leaf", None),
        P("leaf", None),
    )
    return jax.shard_map(
        on_device,
        mesh=mesh,
        in_specs=placed,
        out_specs=P(("leaf", "level"), None, None),
        check_vma=False,
    )
```

time: 107 us -> 105 us (0.981)
  waiting for transfers between devices: 23.4 us -> 25.8 us
  Pallas kernels: 21 us -> 18.7 us
  starting transfers between devices: 32.5 us -> 30.7 us
  local copies, waits for them, and re-layouts: 2.31 us -> 0.9 us
    pallas_call x3, Pallas kernels: 18.1 us -> 14.8 us  [the longest x1 7.16 us: call_near(): pl.pallas_call(near_kernel, out_shape=[pltpu.VMEM((mats.shape[0], 128, 25...]
    ppermute x11, waiting for transfers between devices: 18.2 us -> 20.1 us  [permute(): lax.ppermute(x, axes, pairs)]
    ppermute x11, starting transfers between devices: 27.1 us -> 25.2 us  [permute(): lax.ppermute(x, axes, pairs)]
    unnamed x14 -> x12, local copies, waits for them, and re-layouts: 2.31 us -> 0.9 us
  transfers between devices with their start and end apart: 12 -> 12, of which waited for: 3 -> 3; matrix products, arithmetic and copies ran while one was open for 0% -> 0% of each run, Pallas kernels for 14% -> 13%
where the time goes in v3:
time: 105 us; the launch traced here: 104 us
  starting transfers between devices  30.7 us (29%)
  blocking collectives  27.8 us (26%)
  waiting for transfers between devices  25.8 us (25%)
  Pallas kernels  18.7 us (18%)
    all_to_all x1, blocking collectives, on_device(): lax.all_to_all(message.reshape(256, 4, 128), BOTH, 0, 0, tiled=True)  27.8 us
    ppermute x11, starting transfers between devices, permute(): lax.ppermute(x, axes, pairs)  25.2 us
    ppermute x11, waiting for transfers between devices, permute(): lax.ppermute(x, axes, pairs)  20.1 us
    pallas_call x1, Pallas kernels, call_near(): pl.pallas_call(near_kernel, out_shape=[pltpu.VMEM((mats.shape[0], 128, 25...  7.16 us
    all_to_all x1, waiting for transfers between devices, on_device(): lax.all_to_all(columns.reshape(256, 2, 128), BOTH, 0, 0, tiled=True)  5.68 us
    all_to_all x1, starting transfers between devices, on_device(): lax.all_to_all(columns.reshape(256, 2, 128), BOTH, 0, 0, tiled=True)  5.43 us
    pallas_call x1, Pallas kernels, call_last(): pl.pallas_call(last_kernel, out_shape=jax.ShapeDtypeStruct(near.shape, F3...  4.95 us
    pallas_call x1, Pallas kernels, call_far(): pl.pallas_call(far_kernel, out_shape=jax.ShapeDtypeStruct((512, 128), BF1...  3.82 us
  transfers between devices with their start and end apart: 12, of which 3 were waited for; matrix products, arithmetic and copies ran while one was open for 0% of the time, Pallas kernels for 13%

profile of v3, /device:TPU:1, one launch (start us, length us, event | category | flops | bytes accessed | tf_op | source)
XLA Modules:
  0.0 104.0 jit_solution(15462132498915328054)
XLA Ops:
  0.0 2.1 %collective-permute-start.1 = (bf16[12,128,256]{2,1,0:T(8,128)(2,1)}, bf16[12,128,256]{2,1,0:T(8,128)(2,1)}, u32[]{:S(2)}, u32[]{:S(2)}) collective-permute-start(bf16[12,128,256]{2,1,0:T(8,128)(2,1)} %charges.1), channel_id=1, source_target_pairs={{0,1},{1,2},{2,3},{3,0},{4,5},{5,6},{6,7},{7,4},{8,9},{9,10},{10,1... | collective-permute-start | bytes 2359304 | tf_op jit(solution)/shard_map/ppermute | solution.py:315
  2.1 1.5 %collective-permute-start = (bf16[12,128,256]{2,1,0:T(8,128)(2,1)}, bf16[12,128,256]{2,1,0:T(8,128)(2,1)}, u32[]{:S(2)}, u32[]{:S(2)}) collective-permute-start(bf16[12,128,256]{2,1,0:T(8,128)(2,1)} %charges.1), channel_id=1, source_target_pairs={{1,0},{2,1},{3,2},{0,3},{5,4},{6,5},{7,6},{4,7},{9,8},{10,9},{11,1... | collective-permute-start | bytes 2359304 | tf_op jit(solution)/shard_map/ppermute | solution.py:315
  3.6 2.8 %collective-permute-start.3 = (bf16[12,128,256]{2,1,0:T(8,128)(2,1)}, bf16[12,128,256]{2,1,0:T(8,128)(2,1)}, u32[]{:S(2)}, u32[]{:S(2)}) collective-permute-start(bf16[12,128,256]{2,1,0:T(8,128)(2,1)} %charges.1), channel_id=1, source_target_pairs={{0,4},{1,5},{2,6},{3,7},{4,0},{5,1},{6,2},{7,3},{8,12},{9,13},{10,... | collective-permute-start | bytes 2359304 | tf_op jit(solution)/shard_map/ppermute | solution.py:315
  6.4 1.9 %collective-permute-start.6 = (bf16[12,128,256]{2,1,0:T(8,128)(2,1)}, bf16[12,128,256]{2,1,0:T(8,128)(2,1)S(1)}, u32[]{:S(2)}, u32[]{:S(2)}) collective-permute-start(bf16[12,128,256]{2,1,0:T(8,128)(2,1)} %charges.1), channel_id=1, source_target_pairs={{4,8},{5,9},{6,10},{7,11},{8,4},{9,5},{10,6},{11,7},{12,16},{13,17... | collective-permute-start | bytes 2359304 | tf_op jit(solution)/shard_map/ppermute | solution.py:315
  8.4 10.8 %collective-permute-done.1.refs_3_ = bf16[12,128,256]{2,1,0:T(8,128)(2,1)} collective-permute-done((bf16[12,128,256]{2,1,0:T(8,128)(2,1)}, bf16[12,128,256]{2,1,0:T(8,128)(2,1)}, u32[]{:S(2)}, u32[]{:S(2)}) %collective-permute-start.1) | collective-permute-done | bytes 786464 | tf_op jit(solution)/shard_map/ppermute | solution.py:315
  19.2 1.5 %collective-permute-start.2 = (bf16[12,128,256]{2,1,0:T(8,128)(2,1)}, bf16[12,128,256]{2,1,0:T(8,128)(2,1)}, u32[]{:S(2)}, u32[]{:S(2)}) collective-permute-start(bf16[12,128,256]{2,1,0:T(8,128)(2,1)} %collective-permute-done.1.refs_3_), channel_id=1, source_target_pairs={{0,1},{1,2},{2,3},{3,0},{4,5},{5,6},{6,7},{7,4},{8,9},{9,10},{10,1... | collective-permute-start | bytes 2359304 | tf_op jit(solution)/shard_map/ppermute | solution.py:315
  20.7 0.0 collective-permute-done.refs_1_
  20.7 1.9 %collective-permute-start.4 = (bf16[12,128,256]{2,1,0:T(8,128)(2,1)}, bf16[12,128,256]{2,1,0:T(8,128)(2,1)S(1)}, u32[]{:S(2)}, u32[]{:S(2)}) collective-permute-start(bf16[12,128,256]{2,1,0:T(8,128)(2,1)} %collective-permute-done.refs_1_), channel_id=1, source_target_pairs={{0,4},{1,5},{2,6},{3,7},{4,0},{5,1},{6,2},{7,3},{8,12},{9,13},{10,... | collective-permute-start | bytes 2359304 | tf_op jit(solution)/shard_map/ppermute | solution.py:315
  22.7 0.0 collective-permute-start.5
  22.7 3.5 %collective-permute-start.10 = (bf16[12,128,256]{2,1,0:T(8,128)(2,1)}, bf16[12,128,256]{2,1,0:T(8,128)(2,1)S(1)}, u32[]{:S(2)}, u32[]{:S(2)}) collective-permute-start(bf16[12,128,256]{2,1,0:T(8,128)(2,1)} %collective-permute-done.1.refs_3_), channel_id=1, source_target_pairs={{4,8},{5,9},{6,10},{7,11},{8,4},{9,5},{10,6},{11,7},{12,16},{13,17... | collective-permute-start | bytes 2359304 | tf_op jit(solution)/shard_map/ppermute | solution.py:315
  26.2 2.1 %collective-permute-start.8 = (bf16[12,128,256]{2,1,0:T(8,128)(2,1)}, bf16[12,128,256]{2,1,0:T(8,128)(2,1)}, u32[]{:S(2)}, u32[]{:S(2)}) collective-permute-start(bf16[12,128,256]{2,1,0:T(8,128)(2,1)} %collective-permute-done.refs_1_), channel_id=1, source_target_pairs={{4,8},{5,9},{6,10},{7,11},{8,4},{9,5},{10,6},{11,7},{12,16},{13,17... | collective-permute-start | bytes 2359304 | tf_op jit(solution)/shard_map/ppermute | solution.py:315
  28.3 9.2 %collective-permute-done.2.refs_2_ = bf16[12,128,256]{2,1,0:T(8,128)(2,1)} collective-permute-done((bf16[12,128,256]{2,1,0:T(8,128)(2,1)}, bf16[12,128,256]{2,1,0:T(8,128)(2,1)}, u32[]{:S(2)}, u32[]{:S(2)}) %collective-permute-start.2) | collective-permute-done | bytes 786464 | tf_op jit(solution)/shard_map/ppermute | solution.py:315
  37.5 7.8 %collective-permute-start.9 = (bf16[12,128,256]{2,1,0:T(8,128)(2,1)}, bf16[12,128,256]{2,1,0:T(8,128)(2,1)}, u32[]{:S(2)}, u32[]{:S(2)}) collective-permute-start(bf16[12,128,256]{2,1,0:T(8,128)(2,1)} %collective-permute-done.refs_1_), channel_id=1, source_target_pairs={{4,11},{5,8},{6,9},{7,10},{8,7},{9,4},{10,5},{11,6},{12,19},{13,16... | collective-permute-start | bytes 2359304 | tf_op jit(solution)/shard_map/ppermute | solution.py:315
  45.3 0.0 copy-start.5
  45.3 0.1 collective-permute-start.7
  45.4 2.7 %moment.1 = bf16[1024,128]{1,0:T(8,128)(2,1)} custom-call(bf16[12,128,256]{2,1,0:T(8,128)(2,1)} %charges.1, bf16[12,256,128]{2,1,0:T(8,128)(2,1)} %maps.1, s32[1,32]{1,0:T(1,128)} %cells.1, s32[1,32]{1,0:T(1,128)} %ops.1, s32[1,8]{1,0:T(1,128)} %parents.1, s32[1,8]{1,0:T(1,128)} %parent_ops.1), custom_call_target="tpu_custom_call" | custom-call | tf_op jit(solution)/shard_map/moment/pallas_call | solution.py:250
  48.2 27.8 %all_to_all.10 = bf16[256,4,128]{2,1,0:T(4,128)(2,1)S(1)} all-to-all(bf16[256,4,128]{2,1,0:T(4,128)(2,1)} %bitcast.6), channel_id=1, replica_groups=mesh['leaf'=64,'level'=4] {'leaf','level'}, dimensions={0} | all-to-all | bytes 524288 | tf_op jit(solution)/shard_map/all_to_all | solution.py:370
  76.0 3.8 %far.1 = bf16[512,128]{1,0:T(8,128)(2,1)} custom-call(bf16[1024,128]{1,0:T(8,128)(2,1)S(1)} %bitcast.4, bf16[8,256,256]{2,1,0:T(8,128)(2,1)S(1)} %copy-done, bf16[8,256,256]{2,1,0:T(8,128)(2,1)S(1)} %copy-done.1, bf16[8,256,256]{2,1,0:T(8,128)(2,1)} %shift_hbm.1), custom_call_target="tpu_custom_call" | custom-call | tf_op jit(solution)/shard_map/far/pallas_call | solution.py:262
  79.9 5.4 %all-to-all-start.1 = ((bf16[256,2,128]{2,1,0:T(2,128)(2,1)}), bf16[256,2,128]{2,1,0:T(2,128)(2,1)S(1)}, u32[]{:S(2)}, u32[]{:S(2)}) async-start(bf16[256,2,128]{2,1,0:T(2,128)(2,1)} %bitcast.2), calls=%async_computation.1 | async-start | bytes 262144 | tf_op jit(solution)/shard_map/all_to_all | solution.py:382
  85.3 0.0 copy-start.2
  85.3 7.2 %near.1 = (f32[12,128,256]{2,1,0:T(8,128)S(1)}, s32[3,256]{1,0:T(4,128)}) custom-call(s32[12,16]{1,0:T(8,128)} %sources.1, s32[12]{0:T(128)} %counts.1, bf16[12,128,256]{2,1,0:T(8,128)(2,1)} %charges.1, bf16[12,128,256]{2,1,0:T(8,128)(2,1)} %collective-permute-done.refs_1_, bf16[12,128,256]{2,1,0:T(8,128)(2,1)} %collective-permute-done.2.refs_2_, ...), custom_call_target="tpu_custom_call" | custom-call | tf_op jit(solution)/shard_map/near/pallas_call | solution.py:278
  92.5 5.7 %all-to-all-done.1 = bf16[256,2,128]{2,1,0:T(2,128)(2,1)S(1)} async-done(((bf16[256,2,128]{2,1,0:T(2,128)(2,1)}), bf16[256,2,128]{2,1,0:T(2,128)(2,1)S(1)}, u32[]{:S(2)}, u32[]{:S(2)}) %all-to-all-start.1) | async-done | bytes 131104 | tf_op jit(solution)/shard_map/all_to_all | solution.py:382
  98.2 0.9 copy-done.3
  99.1 4.9 %last.1 = f32[12,128,256]{2,1,0:T(8,128)} custom-call(s32[3,256]{1,0:T(4,128)} %get-tuple-element.7.late, bf16[12,128,256]{2,1,0:T(8,128)(2,1)} %collective-permute-done.7.refs_0_, bf16[12,128,256]{2,1,0:T(8,128)(2,1)} %collective-permute-done.8.refs_1_, bf16[12,128,256]{2,1,0:T(8,128)(2,1)} %collective-permute-done.9.refs_2_, ...), custom_call_target="tpu_custom_call" | custom-call | tf_op jit(solution)/shard_map/last/pallas_call | solution.py:296
  (17 shorter events, 0.0 us)
Async XLA Ops:
  0.0 76.0 %copy-start = (bf16[8,256,256]{2,1,0:T(8,128)(2,1)S(1)}, bf16[8,256,256]{2,1,0:T(8,128)(2,1)}, u32[]{:S(2)}) copy-start(bf16[8,256,256]{2,1,0:T(8,128)(2,1)} %upward.1) | copy-start | bytes 3145732
  0.0 76.0 %copy-start.1 = (bf16[8,256,256]{2,1,0:T(8,128)(2,1)S(1)}, bf16[8,256,256]{2,1,0:T(8,128)(2,1)}, u32[]{:S(2)}) copy-start(bf16[8,256,256]{2,1,0:T(8,128)(2,1)} %transfer.1) | copy-start | bytes 3145732
  0.0 19.2 %collective-permute-start.1 = (bf16[12,128,256]{2,1,0:T(8,128)(2,1)}, bf16[12,128,256]{2,1,0:T(8,128)(2,1)}, u32[]{:S(2)}, u32[]{:S(2)}) collective-permute-start(bf16[12,128,256]{2,1,0:T(8,128)(2,1)} %charges.1), channel_id=1, source_target_pairs={{0,1},{1,2},{2,3},{3,0},{4,5},{5,6},{6,7},{7,4},{8,9},{9,10},{10,1... | collective-permute-start | bytes 2359304 | tf_op jit(solution)/shard_map/ppermute | solution.py:315
  2.1 18.6 %collective-permute-start = (bf16[12,128,256]{2,1,0:T(8,128)(2,1)}, bf16[12,128,256]{2,1,0:T(8,128)(2,1)}, u32[]{:S(2)}, u32[]{:S(2)}) collective-permute-start(bf16[12,128,256]{2,1,0:T(8,128)(2,1)} %charges.1), channel_id=1, source_target_pairs={{1,0},{2,1},{3,2},{0,3},{5,4},{6,5},{7,6},{4,7},{9,8},{10,9},{11,1... | collective-permute-start | bytes 2359304 | tf_op jit(solution)/shard_map/ppermute | solution.py:315
  3.6 19.0 %collective-permute-start.3 = (bf16[12,128,256]{2,1,0:T(8,128)(2,1)}, bf16[12,128,256]{2,1,0:T(8,128)(2,1)}, u32[]{:S(2)}, u32[]{:S(2)}) collective-permute-start(bf16[12,128,256]{2,1,0:T(8,128)(2,1)} %charges.1), channel_id=1, source_target_pairs={{0,4},{1,5},{2,6},{3,7},{4,0},{5,1},{6,2},{7,3},{8,12},{9,13},{10,... | collective-permute-start | bytes 2359304 | tf_op jit(solution)/shard_map/ppermute | solution.py:315
  6.4 19.8 %collective-permute-start.6 = (bf16[12,128,256]{2,1,0:T(8,128)(2,1)}, bf16[12,128,256]{2,1,0:T(8,128)(2,1)S(1)}, u32[]{:S(2)}, u32[]{:S(2)}) collective-permute-start(bf16[12,128,256]{2,1,0:T(8,128)(2,1)} %charges.1), channel_id=1, source_target_pairs={{4,8},{5,9},{6,10},{7,11},{8,4},{9,5},{10,6},{11,7},{12,16},{13,17... | collective-permute-start | bytes 2359304 | tf_op jit(solution)/shard_map/ppermute | solution.py:315
  19.2 18.3 %collective-permute-start.2 = (bf16[12,128,256]{2,1,0:T(8,128)(2,1)}, bf16[12,128,256]{2,1,0:T(8,128)(2,1)}, u32[]{:S(2)}, u32[]{:S(2)}) collective-permute-start(bf16[12,128,256]{2,1,0:T(8,128)(2,1)} %collective-permute-done.1.refs_3_), channel_id=1, source_target_pairs={{0,1},{1,2},{2,3},{3,0},{4,5},{5,6},{6,7},{7,4},{8,9},{9,10},{10,1... | collective-permute-start | bytes 2359304 | tf_op jit(solution)/shard_map/ppermute | solution.py:315
  20.7 24.6 %collective-permute-start.4 = (bf16[12,128,256]{2,1,0:T(8,128)(2,1)}, bf16[12,128,256]{2,1,0:T(8,128)(2,1)S(1)}, u32[]{:S(2)}, u32[]{:S(2)}) collective-permute-start(bf16[12,128,256]{2,1,0:T(8,128)(2,1)} %collective-permute-done.refs_1_), channel_id=1, source_target_pairs={{0,4},{1,5},{2,6},{3,7},{4,0},{5,1},{6,2},{7,3},{8,12},{9,13},{10,... | collective-permute-start | bytes 2359304 | tf_op jit(solution)/shard_map/ppermute | solution.py:315
  22.7 62.6 %collective-permute-start.5 = (bf16[12,128,256]{2,1,0:T(8,128)(2,1)}, bf16[12,128,256]{2,1,0:T(8,128)(2,1)}, u32[]{:S(2)}, u32[]{:S(2)}) collective-permute-start(bf16[12,128,256]{2,1,0:T(8,128)(2,1)} %collective-permute-done.1.refs_3_), channel_id=1, source_target_pairs={{0,4},{1,5},{2,6},{3,7},{4,0},{5,1},{6,2},{7,3},{8,12},{9,13},{10,... | collective-permute-start | bytes 2359304 | tf_op jit(solution)/shard_map/ppermute | solution.py:315
  22.7 75.5 %collective-permute-start.10 = (bf16[12,128,256]{2,1,0:T(8,128)(2,1)}, bf16[12,128,256]{2,1,0:T(8,128)(2,1)S(1)}, u32[]{:S(2)}, u32[]{:S(2)}) collective-permute-start(bf16[12,128,256]{2,1,0:T(8,128)(2,1)} %collective-permute-done.1.refs_3_), channel_id=1, source_target_pairs={{4,8},{5,9},{6,10},{7,11},{8,4},{9,5},{10,6},{11,7},{12,16},{13,17... | collective-permute-start | bytes 2359304 | tf_op jit(solution)/shard_map/ppermute | solution.py:315
  26.2 53.6 %copy-start.4 = (bf16[12,128,256]{2,1,0:T(8,128)(2,1)}, bf16[12,128,256]{2,1,0:T(8,128)(2,1)S(1)}, u32[]{:S(2)}) copy-start(bf16[12,128,256]{2,1,0:T(8,128)(2,1)S(1)} %collective-permute-done.6.refs_7_) | copy-start | bytes 2359300
  26.2 72.0 %collective-permute-start.8 = (bf16[12,128,256]{2,1,0:T(8,128)(2,1)}, bf16[12,128,256]{2,1,0:T(8,128)(2,1)}, u32[]{:S(2)}, u32[]{:S(2)}) collective-permute-start(bf16[12,128,256]{2,1,0:T(8,128)(2,1)} %collective-permute-done.refs_1_), channel_id=1, source_target_pairs={{4,8},{5,9},{6,10},{7,11},{8,4},{9,5},{10,6},{11,7},{12,16},{13,17... | collective-permute-start | bytes 2359304 | tf_op jit(solution)/shard_map/ppermute | solution.py:315
  37.5 60.7 %collective-permute-start.9 = (bf16[12,128,256]{2,1,0:T(8,128)(2,1)}, bf16[12,128,256]{2,1,0:T(8,128)(2,1)}, u32[]{:S(2)}, u32[]{:S(2)}) collective-permute-start(bf16[12,128,256]{2,1,0:T(8,128)(2,1)} %collective-permute-done.refs_1_), channel_id=1, source_target_pairs={{4,11},{5,8},{6,9},{7,10},{8,7},{9,4},{10,5},{11,6},{12,19},{13,16... | collective-permute-start | bytes 2359304 | tf_op jit(solution)/shard_map/ppermute | solution.py:315
  45.3 34.6 %copy-start.5 = (bf16[12,128,256]{2,1,0:T(8,128)(2,1)}, bf16[12,128,256]{2,1,0:T(8,128)(2,1)S(1)}, u32[]{:S(2)}) copy-start(bf16[12,128,256]{2,1,0:T(8,128)(2,1)S(1)} %collective-permute-done.4.refs_5_) | copy-start | bytes 2359300
  45.3 52.9 %collective-permute-start.7 = (bf16[12,128,256]{2,1,0:T(8,128)(2,1)}, bf16[12,128,256]{2,1,0:T(8,128)(2,1)}, u32[]{:S(2)}, u32[]{:S(2)}) collective-permute-start(bf16[12,128,256]{2,1,0:T(8,128)(2,1)} %collective-permute-done.2.refs_2_), channel_id=1, source_target_pairs={{0,4},{1,5},{2,6},{3,7},{4,0},{5,1},{6,2},{7,3},{8,12},{9,13},{10,... | collective-permute-start | bytes 2359304 | tf_op jit(solution)/shard_map/ppermute | solution.py:315
  79.9 18.3 %all-to-all-start.1 = ((bf16[256,2,128]{2,1,0:T(2,128)(2,1)}), bf16[256,2,128]{2,1,0:T(2,128)(2,1)S(1)}, u32[]{:S(2)}, u32[]{:S(2)}) async-start(bf16[256,2,128]{2,1,0:T(2,128)(2,1)} %bitcast.2), calls=%async_computation.1 | async-start | bytes 262144 | tf_op jit(solution)/shard_map/all_to_all | solution.py:382
  85.3 13.8 %copy-start.2 = (bf16[12,128,256]{2,1,0:T(8,128)(2,1)S(1)}, bf16[12,128,256]{2,1,0:T(8,128)(2,1)}, u32[]{:S(2)}) copy-start(bf16[12,128,256]{2,1,0:T(8,128)(2,1)} %refs_6_.1) | copy-start | bytes 2359300
  98.2 0.9 copy-start.3
